TPU v7x, 32 devices: a whole 2x2x4 slice. The times are simulated.
32 devices in a mesh: section: 4 (over y, core), dp: 4 (over z), tensor: 2 (over x).
Axes of the slice: x: 2, y: 2, z: 4, core: 2. Of those that a mesh axis runs over, the one named last changes fastest.
Arguments:
- query_embedded: bfloat16 [16, 4096], P('dp'), may hold values from -6 to 6
- passage_embedded: bfloat16 [48, 4096], P('dp'), may hold values from -6 to 6
- positives: int32 [16], P('dp'), may hold values from 0 to 47
- counts: int32 [16], P('dp'), may hold values from 1 to 32, as said below
- stored_inputs: bfloat16 [4, 512, 4096], P('section', 'dp', 'tensor'), may hold values from -6 to 6
- adapter_inner: bfloat16 [4, 512, 16], P('section', 'dp'), may hold values from -6 to 6
- branch_slope: bfloat16 [4, 512, 4096], P('section', 'dp', 'tensor'), may hold values from -6 to 6
- frozen_projection: bfloat16 [4, 4096, 4096], P('section', None, 'tensor'), may hold values from -0.046875 to 0.046875
- adapter_down: bfloat16 [4, 4096, 16], P('section', 'tensor'), may hold values from -0.09375 to 0.09375
- adapter_up: bfloat16 [4, 16, 4096], P('section', None, 'tensor'), may hold values from -0.09375 to 0.09375
Outputs:
- grad_inputs: bfloat16 [4, 512, 4096], P('section', 'dp', 'tensor')
- adapter_grads: float32 [4, 32, 4096], P('section', 'dp', 'tensor')
Inputs may be any that keep to these rules, and one draw needn't show every extreme that they name: Query i's live tokens are its first counts[i] rows of 32; some query has all 32.
All inputs are finite; a program needn't handle non-finite values.
Results may differ from a plain program's by a relative error of at most 0.017.
Values may be sent and summed in bfloat16 or wider, within the bound.
No kernel may reach another device: no remote copies, remote signals or barrier semaphores. Data moves between devices by JAX's collectives and lax.ppermute only.
A program may use at most 64 MiB of HBM per device.

v0:
```python
import math

import jax
import jax.numpy as jnp
from jax import lax
from jax.sharding import PartitionSpec as P

ADAPTER_SCALE = 2.0
LOSS_SCALE = 32.0


def shifted(value, axis, steps):
    count = lax.axis_size(axis)
    first, last = (max(0, -steps), min(count, count - steps))
    return lax.ppermute(value, axis, [(source, source + steps) for source in range(first, last)])


def shards(
    query_embedded,
    passage_embedded,
    positives,
    counts,
    stored_inputs,
    adapter_inner,
    branch_slope,
    frozen_projection,
    adapter_down,
    adapter_up,
):
    section_count = lax.axis_size("section")
    tensor_count = lax.axis_size("tensor")
    replica_total = lax.axis_size("dp")
    section_index = lax.axis_index("section")
    tensor_index = lax.axis_index("tensor")
    microbatch_count = query_embedded.shape[0]
    model_width = query_embedded.shape[1]
    local_width = model_width // tensor_count
    rank_total = adapter_up.shape[1]
    query_length = stored_inputs.shape[1] // microbatch_count
    inverse_root = 1.0 / math.sqrt(model_width)
    column_start = tensor_index * local_width
    shard_piece = lax.all_gather(passage_embedded, "dp", axis=0, tiled=True)
    scores = (
        jnp.dot(query_embedded, shard_piece.T, preferred_element_type=jnp.float32) * inverse_root
    )
    columns = jnp.arange(shard_piece.shape[0], dtype=jnp.int32)
    target = (positives[:, None] == columns[None, :]).astype(jnp.float32)
    score_grad = (jax.nn.sigmoid(scores) - target).astype(jnp.bfloat16)
    piece_cols = lax.dynamic_slice_in_dim(shard_piece, column_start, local_width, 1)
    query_sum = jnp.dot(score_grad, piece_cols, preferred_element_type=jnp.float32)
    query_grad = query_sum * inverse_root
    positions = jnp.arange(query_length, dtype=jnp.int32)
    live_mask = (positions[None, :] < counts[:, None]).astype(jnp.float32)
    token_scale = live_mask * (LOSS_SCALE / counts.astype(jnp.float32))[:, None]
    top_grad = (
        (query_grad[:, None, :] * token_scale[:, :, None])
        .reshape(microbatch_count * query_length, local_width)
        .astype(jnp.bfloat16)
    )
    group_size = 2
    group_count = microbatch_count // group_size
    block_rows = group_size * query_length
    step_count = group_count + section_count - 1
    frozen_local = frozen_projection[0]
    down_shard = adapter_down[0]
    up_shard = adapter_up[0]
    input_local = stored_inputs[0]
    inner_shard = adapter_inner[0]
    slope_local = branch_slope[0]
    section_delay = section_count - 1 - section_index
    last_section = section_index == section_count - 1
    contract_last = (((1,), (1,)), ((), ()))

    def local_terms(branch_block):
        frozen_part = lax.dot_general(
            branch_block, frozen_local, contract_last, preferred_element_type=jnp.float32
        )
        inner_part = lax.dot_general(
            branch_block, up_shard, contract_last, preferred_element_type=jnp.float32
        )
        return (frozen_part, jnp.tile(inner_part, (1, tensor_count)))

    def empty_terms(branch_block):
        return (
            jnp.zeros((block_rows, model_width), jnp.float32),
            jnp.zeros((block_rows, rank_total * tensor_count), jnp.float32),
        )

    def section_step(step_index, carry):
        outgoing, results, down_total, up_total = carry
        incoming = shifted(outgoing, "section", -1)
        group_index = step_index - section_delay
        active_flag = (group_index >= 0) & (group_index < group_count)
        group_safe = jnp.clip(group_index, 0, group_count - 1)
        row_start = group_safe * block_rows
        top_block = lax.dynamic_slice_in_dim(top_grad, row_start, block_rows, 0)
        gradient_block = jnp.where(last_section, top_block, incoming)
        slope_block = lax.dynamic_slice_in_dim(slope_local, row_start, block_rows, 0)
        branch_block = (
            gradient_block.astype(jnp.float32) * slope_block.astype(jnp.float32)
        ).astype(jnp.bfloat16)
        frozen_part, inner_tiles = lax.cond(active_flag, local_terms, empty_terms, branch_block)
        frozen_total, inner_total = (
            lax.psum_scatter(
                frozen_part.astype(jnp.bfloat16), "tensor", scatter_dimension=1, tiled=True
            ).astype(jnp.float32),
            lax.psum_scatter(
                inner_tiles.astype(jnp.bfloat16), "tensor", scatter_dimension=1, tiled=True
            ).astype(jnp.float32),
        )
        inner_rows_block = inner_total.astype(jnp.bfloat16)
        adapter_term = ADAPTER_SCALE * jnp.dot(
            inner_rows_block, down_shard.T, preferred_element_type=jnp.float32
        )
        gradient_next = (gradient_block.astype(jnp.float32) + frozen_total + adapter_term).astype(
            jnp.bfloat16
        )
        input_block = lax.dynamic_slice_in_dim(input_local, row_start, block_rows, 0)
        saved_inner = lax.dynamic_slice_in_dim(inner_shard, row_start, block_rows, 0)
        active_gate = active_flag.astype(jnp.float32)
        down_total = down_total + active_gate * jnp.dot(
            inner_rows_block.T, input_block, preferred_element_type=jnp.float32
        )
        up_total = up_total + active_gate * jnp.dot(
            saved_inner.T, branch_block, preferred_element_type=jnp.float32
        )
        previous = lax.dynamic_slice_in_dim(results, row_start, block_rows, 0)
        results = lax.dynamic_update_slice_in_dim(
            results, jnp.where(active_flag, gradient_next, previous), row_start, 0
        )
        return (gradient_next, results, down_total, up_total)

    start_carry = (
        jnp.zeros((block_rows, local_width), jnp.bfloat16),
        jnp.zeros((microbatch_count * query_length, local_width), jnp.bfloat16),
        jnp.zeros((rank_total, local_width), jnp.float32),
        jnp.zeros((rank_total, local_width), jnp.float32),
    )
    unused, results, down_total, up_total = lax.fori_loop(0, step_count, section_step, start_carry)
    adapter_factor = ADAPTER_SCALE / (microbatch_count * replica_total)
    adapter_local = jnp.concatenate([down_total, up_total], axis=0) * adapter_factor
    reduced = lax.psum_scatter(
        adapter_local.astype(jnp.bfloat16), "dp", scatter_dimension=0, tiled=True
    ).astype(jnp.float32)
    return (results[None], reduced[None])


def solution(mesh):
    return jax.shard_map(
        shards,
        mesh=mesh,
        in_specs=(
            P("dp", None),
            P("dp", None),
            P("dp"),
            P("dp"),
            P("section", "dp", "tensor"),
            P("section", "dp", None),
            P("section", "dp", "tensor"),
            P("section", None, "tensor"),
            P("section", "tensor", None),
            P("section", None, "tensor"),
        ),
        out_specs=(P("section", "dp", "tensor"), P("section", "dp", "tensor")),
        check_vma=False,
    )
```

profile of v0, /device:TPU:0, one launch (start us, length us, event | category | flops | bytes accessed | tf_op | source)
XLA Modules:
  0.0 294.9 jit_solution(4230305786839919583)
XLA Ops:
  8.1 17.6 %all-gather = bf16[4,12,4096]{2,1,0:T(8,128)(2,1)S(1)} all-gather(bf16[1,12,4096]{2,1,0:T(8,128)(2,1)} %bitcast.41), channel_id=1, replica_groups=mesh['section'=4,'dp'=4,'tensor'=2] {'dp'}, dimensions={0}, use_global_device_ids=true | all-gather | bytes 491520 | tf_op jit(solution)/shard_map/all_gather | solution.py:42
  25.7 0.7 convert_divide_fusion
  26.4 0.7 fusion.19
  27.2 1.1 convolution_multiply_fusion.3
  28.5 235.4 %while.20 = (s32[]{:T(128)}, bf16[64,2048]{1,0:T(8,128)(2,1)S(1)}, bf16[128,2048]{1,0:T(8,128)(2,1)S(1)}, f32[16,2048]{1,0:T(8,128)S(1)}, f32[16,2048]{1,0:T(8,1...) while((s32[]{:T(128)}, bf16[64,2048]{1,0:T(8,128)(2,1)S(1)}, ...), condition=%wide.region_5.6_spmd.clone, body=%wide.region_0.5_spmd.clone.sunk | while | flops 1092550656 | bytes 30352012 | solution.py:139
  28.6 1.4 collective-permute-start
  30.1 2.1 collective-permute-done
  32.2 1.0 fusion.53
  34.9 21.8 %reduce-scatter.6.cloned.1.call-done = bf16[64,16]{0,1:T(8,128)(2,1)} async-done(((bf16[64,32]{0,1:T(8,128)(2,1)}), bf16[64,16]{0,1:T(8,128)(2,1)}) %reduce-scatter.6.cloned.1.call-update) | async-done | bytes 2064 | tf_op jit(solution)/shard_map/while/body/eval_jaxpr/reduce_scatter | solution.py:107
  56.7 0.8 fusion.54
  57.6 16.6 %reduce-scatter.8.cloned.1.call-done = bf16[64,2048]{1,0:T(8,128)(2,1)} async-done(((bf16[64,4096]{1,0:T(8,128)(2,1)}), bf16[64,2048]{1,0:T(8,128)(2,1)}) %reduce-scatter.8.cloned.1.call-update) | async-done | bytes 262160 | tf_op jit(solution)/shard_map/while/body/eval_jaxpr/reduce_scatter | solution.py:104
  74.2 1.2 select_dynamic-update-slice_fusion.2
  75.6 1.4 collective-permute-start
  77.0 2.1 collective-permute-done
  79.1 1.0 fusion.53
  81.7 22.8 %reduce-scatter.6.cloned.1.call-done = bf16[64,16]{0,1:T(8,128)(2,1)} async-done(((bf16[64,32]{0,1:T(8,128)(2,1)}), bf16[64,16]{0,1:T(8,128)(2,1)}) %reduce-scatter.6.cloned.1.call-update) | async-done | bytes 2064 | tf_op jit(solution)/shard_map/while/body/eval_jaxpr/reduce_scatter | solution.py:107
  104.5 0.8 fusion.54
  105.3 16.5 %reduce-scatter.8.cloned.1.call-done = bf16[64,2048]{1,0:T(8,128)(2,1)} async-done(((bf16[64,4096]{1,0:T(8,128)(2,1)}), bf16[64,2048]{1,0:T(8,128)(2,1)}) %reduce-scatter.8.cloned.1.call-update) | async-done | bytes 262160 | tf_op jit(solution)/shard_map/while/body/eval_jaxpr/reduce_scatter | solution.py:104
  121.8 1.3 select_dynamic-update-slice_fusion.2
  123.2 1.4 collective-permute-start
  124.7 2.1 collective-permute-done
  126.8 1.0 fusion.53
  129.4 23.3 %reduce-scatter.6.cloned.1.call-done = bf16[64,16]{0,1:T(8,128)(2,1)} async-done(((bf16[64,32]{0,1:T(8,128)(2,1)}), bf16[64,16]{0,1:T(8,128)(2,1)}) %reduce-scatter.6.cloned.1.call-update) | async-done | bytes 2064 | tf_op jit(solution)/shard_map/while/body/eval_jaxpr/reduce_scatter | solution.py:107
  152.7 0.8 fusion.54
  153.5 16.5 %reduce-scatter.8.cloned.1.call-done = bf16[64,2048]{1,0:T(8,128)(2,1)} async-done(((bf16[64,4096]{1,0:T(8,128)(2,1)}), bf16[64,2048]{1,0:T(8,128)(2,1)}) %reduce-scatter.8.cloned.1.call-update) | async-done | bytes 262160 | tf_op jit(solution)/shard_map/while/body/eval_jaxpr/reduce_scatter | solution.py:104
  170.0 1.3 select_dynamic-update-slice_fusion.2
  171.4 1.4 collective-permute-start
  172.9 2.1 collective-permute-done
  175.0 1.0 fusion.53
  176.0 11.2 %conditional.3 = (bf16[64,4096]{1,0:T(8,128)(2,1)S(1)}, bf16[64,32]{0,1:T(8,128)(2,1)S(1)}) conditional(s32[]{:T(128)} %convert_element_type.131, () %tuple.51, (bf16[64,2048]{1,0:T(8,128)(2,1)S(1)}, bf16[4096,2048]{1,0:T(8,128)(2,1)}, bf16[16,2048]{1,0:T(8,128)(2,1)}) %tuple.52), branch_computations={%region_1.1_spmd, %region_2.2_spmd} | conditional | flops 1077936128 | bytes 18161708 | solution.py:102
  176.1 11.0 %fusion.26 = bf16[64,4096]{1,0:T(8,128)(2,1)S(1)} fusion(bf16[64,2048]{1,0:T(8,128)(2,1)S(1)} %get-tuple-element.219, bf16[4096,2048]{1,0:T(8,128)(2,1)} %get-tuple-element.220), kind=kOutput, calls=%fused_computation.42 | convolution fusion | flops 1073741824 | bytes 17563648 | tf_op jit(solution)/shard_map/while/body/eval_jaxpr/cond/branch_1_fun/dot_general | solution.py:75
  187.2 0.6 copy-done.6
  188.9 11.9 %reduce-scatter.6.cloned.1.call-done = bf16[64,16]{0,1:T(8,128)(2,1)} async-done(((bf16[64,32]{0,1:T(8,128)(2,1)}), bf16[64,16]{0,1:T(8,128)(2,1)}) %reduce-scatter.6.cloned.1.call-update) | async-done | bytes 2064 | tf_op jit(solution)/shard_map/while/body/eval_jaxpr/reduce_scatter | solution.py:107
  200.8 0.8 fusion.54
  201.6 16.6 %reduce-scatter.8.cloned.1.call-done = bf16[64,2048]{1,0:T(8,128)(2,1)} async-done(((bf16[64,4096]{1,0:T(8,128)(2,1)}), bf16[64,2048]{1,0:T(8,128)(2,1)}) %reduce-scatter.8.cloned.1.call-update) | async-done | bytes 262160 | tf_op jit(solution)/shard_map/while/body/eval_jaxpr/reduce_scatter | solution.py:104
  218.3 1.2 select_dynamic-update-slice_fusion.2
  219.7 1.4 collective-permute-start
  221.1 2.1 collective-permute-done
  223.2 1.0 fusion.53
  224.3 11.2 %conditional.3 = (bf16[64,4096]{1,0:T(8,128)(2,1)S(1)}, bf16[64,32]{0,1:T(8,128)(2,1)S(1)}) conditional(s32[]{:T(128)} %convert_element_type.131, () %tuple.51, (bf16[64,2048]{1,0:T(8,128)(2,1)S(1)}, bf16[4096,2048]{1,0:T(8,128)(2,1)}, bf16[16,2048]{1,0:T(8,128)(2,1)}) %tuple.52), branch_computations={%region_1.1_spmd, %region_2.2_spmd} | conditional | flops 1077936128 | bytes 18161708 | solution.py:102
  224.3 11.0 %fusion.26 = bf16[64,4096]{1,0:T(8,128)(2,1)S(1)} fusion(bf16[64,2048]{1,0:T(8,128)(2,1)S(1)} %get-tuple-element.219, bf16[4096,2048]{1,0:T(8,128)(2,1)} %get-tuple-element.220), kind=kOutput, calls=%fused_computation.42 | convolution fusion | flops 1073741824 | bytes 17563648 | tf_op jit(solution)/shard_map/while/body/eval_jaxpr/cond/branch_1_fun/dot_general | solution.py:75
  237.0 8.3 %reduce-scatter.6.cloned.1.call-done = bf16[64,16]{0,1:T(8,128)(2,1)} async-done(((bf16[64,32]{0,1:T(8,128)(2,1)}), bf16[64,16]{0,1:T(8,128)(2,1)}) %reduce-scatter.6.cloned.1.call-update) | async-done | bytes 2064 | tf_op jit(solution)/shard_map/while/body/eval_jaxpr/reduce_scatter | solution.py:107
  245.3 0.8 fusion.54
  246.1 16.5 %reduce-scatter.8.cloned.1.call-done = bf16[64,2048]{1,0:T(8,128)(2,1)} async-done(((bf16[64,4096]{1,0:T(8,128)(2,1)}), bf16[64,2048]{1,0:T(8,128)(2,1)}) %reduce-scatter.8.cloned.1.call-update) | async-done | bytes 262160 | tf_op jit(solution)/shard_map/while/body/eval_jaxpr/reduce_scatter | solution.py:104
  262.6 1.3 select_dynamic-update-slice_fusion.2
  264.0 0.8 fusion.16
  264.8 21.3 %reduce-scatter.4.cloned.1.call-done = bf16[8,2048]{1,0:T(8,128)(2,1)} async-done(((bf16[32,2048]{1,0:T(8,128)(2,1)}), bf16[8,2048]{1,0:T(8,128)(2,1)}) %reduce-scatter.4.cloned.1.call-update) | async-done | bytes 32784 | tf_op jit(solution)/shard_map/reduce_scatter | solution.py:142
  286.1 1.4 bitcast_convert_fusion
  (109 shorter events, 8.3 us)
Async XLA Ops:
  8.0 19.2 %copy-start = (bf16[4,4096]{1,0:T(4,128)(2,1)S(1)}, bf16[4,4096]{1,0:T(4,128)(2,1)}, u32[]{:S(2)}) copy-start(bf16[4,4096]{1,0:T(4,128)(2,1)} %param.14) | copy-start | bytes 98308
  28.5 6.2 %copy-start.7 = (bf16[128,16]{0,1:T(8,128)(2,1)S(1)}, bf16[128,16]{0,1:T(8,128)(2,1)}, u32[]{:S(2)}) copy-start(bf16[128,16]{0,1:T(8,128)(2,1)} %get-tuple-element.472) | copy-start | bytes 12292 | tf_op jit(solution)/shard_map/while
  28.5 28.2 %copy-start.3 = (bf16[128,2048]{1,0:T(8,128)(2,1)S(1)}, bf16[128,2048]{1,0:T(8,128)(2,1)}, u32[]{:S(2)}) copy-start(bf16[128,2048]{1,0:T(8,128)(2,1)} %get-tuple-element.471) | copy-start | bytes 1572868 | tf_op jit(solution)/shard_map/while
  28.5 45.7 %copy-start.5 = (bf16[2048,16]{0,1:T(8,128)(2,1)S(1)}, bf16[2048,16]{0,1:T(8,128)(2,1)}, u32[]{:S(2)}) copy-start(bf16[2048,16]{0,1:T(8,128)(2,1)} %get-tuple-element.470) | copy-start | bytes 196612 | tf_op jit(solution)/shard_map/while
  28.5 28.2 %reduce-scatter.6.cloned.1.call-start = ((), (), s32[]{:S(2)}) async-start(), calls=%async_computation.4 | async-start | bytes 12288 | tf_op jit(solution)/shard_map/while/body/eval_jaxpr/reduce_scatter | solution.py:107
  28.6 3.6 %collective-permute-start = (bf16[64,2048]{1,0:T(8,128)(2,1)S(1)}, bf16[64,2048]{1,0:T(8,128)(2,1)S(1)}, u32[]{:S(2)}, u32[]{:S(2)}) collective-permute-start(bf16[64,2048]{1,0:T(8,128)(2,1)S(1)} %broadcast_select_fusion.2), channel_id=1, source_target_pairs={{8,0},{16,8},{24,16},{9,1},{17,9},{25,17},{10,2},{18,10},{26,18},{... | collective-permute-start | bytes 786440 | tf_op jit(solution)/shard_map/while/body/eval_jaxpr/ppermute | solution.py:15
  33.3 0.6 copy-start.6
  33.3 0.8 copy-start.1
  33.9 40.2 %reduce-scatter.8.cloned.1.call-start = ((), (), s32[]{:S(2)}) async-start(), calls=%async_computation.5 | async-start | bytes 786432 | tf_op jit(solution)/shard_map/while/body/eval_jaxpr/reduce_scatter | solution.py:104
  75.4 6.0 %copy-start.7 = (bf16[128,16]{0,1:T(8,128)(2,1)S(1)}, bf16[128,16]{0,1:T(8,128)(2,1)}, u32[]{:S(2)}) copy-start(bf16[128,16]{0,1:T(8,128)(2,1)} %get-tuple-element.472) | copy-start | bytes 12292 | tf_op jit(solution)/shard_map/while
  75.4 29.0 %copy-start.3 = (bf16[128,2048]{1,0:T(8,128)(2,1)S(1)}, bf16[128,2048]{1,0:T(8,128)(2,1)}, u32[]{:S(2)}) copy-start(bf16[128,2048]{1,0:T(8,128)(2,1)} %get-tuple-element.471) | copy-start | bytes 1572868 | tf_op jit(solution)/shard_map/while
  75.5 46.4 %copy-start.5 = (bf16[2048,16]{0,1:T(8,128)(2,1)S(1)}, bf16[2048,16]{0,1:T(8,128)(2,1)}, u32[]{:S(2)}) copy-start(bf16[2048,16]{0,1:T(8,128)(2,1)} %get-tuple-element.470) | copy-start | bytes 196612 | tf_op jit(solution)/shard_map/while
  75.5 29.0 %reduce-scatter.6.cloned.1.call-start = ((), (), s32[]{:S(2)}) async-start(), calls=%async_computation.4 | async-start | bytes 12288 | tf_op jit(solution)/shard_map/while/body/eval_jaxpr/reduce_scatter | solution.py:107
  75.6 3.6 %collective-permute-start = (bf16[64,2048]{1,0:T(8,128)(2,1)S(1)}, bf16[64,2048]{1,0:T(8,128)(2,1)S(1)}, u32[]{:S(2)}, u32[]{:S(2)}) collective-permute-start(bf16[64,2048]{1,0:T(8,128)(2,1)S(1)} %broadcast_select_fusion.2), channel_id=1, source_target_pairs={{8,0},{16,8},{24,16},{9,1},{17,9},{25,17},{10,2},{18,10},{26,18},{... | collective-permute-start | bytes 786440 | tf_op jit(solution)/shard_map/while/body/eval_jaxpr/ppermute | solution.py:15
  80.3 0.6 copy-start.6
  80.3 0.8 copy-start.1
  80.9 40.9 %reduce-scatter.8.cloned.1.call-start = ((), (), s32[]{:S(2)}) async-start(), calls=%async_computation.5 | async-start | bytes 786432 | tf_op jit(solution)/shard_map/while/body/eval_jaxpr/reduce_scatter | solution.py:104
  123.1 6.0 %copy-start.7 = (bf16[128,16]{0,1:T(8,128)(2,1)S(1)}, bf16[128,16]{0,1:T(8,128)(2,1)}, u32[]{:S(2)}) copy-start(bf16[128,16]{0,1:T(8,128)(2,1)} %get-tuple-element.472) | copy-start | bytes 12292 | tf_op jit(solution)/shard_map/while
  123.1 29.6 %copy-start.3 = (bf16[128,2048]{1,0:T(8,128)(2,1)S(1)}, bf16[128,2048]{1,0:T(8,128)(2,1)}, u32[]{:S(2)}) copy-start(bf16[128,2048]{1,0:T(8,128)(2,1)} %get-tuple-element.471) | copy-start | bytes 1572868 | tf_op jit(solution)/shard_map/while
  123.1 46.9 %copy-start.5 = (bf16[2048,16]{0,1:T(8,128)(2,1)S(1)}, bf16[2048,16]{0,1:T(8,128)(2,1)}, u32[]{:S(2)}) copy-start(bf16[2048,16]{0,1:T(8,128)(2,1)} %get-tuple-element.470) | copy-start | bytes 196612 | tf_op jit(solution)/shard_map/while
  123.1 29.5 %reduce-scatter.6.cloned.1.call-start = ((), (), s32[]{:S(2)}) async-start(), calls=%async_computation.4 | async-start | bytes 12288 | tf_op jit(solution)/shard_map/while/body/eval_jaxpr/reduce_scatter | solution.py:107
  123.2 3.6 %collective-permute-start = (bf16[64,2048]{1,0:T(8,128)(2,1)S(1)}, bf16[64,2048]{1,0:T(8,128)(2,1)S(1)}, u32[]{:S(2)}, u32[]{:S(2)}) collective-permute-start(bf16[64,2048]{1,0:T(8,128)(2,1)S(1)} %broadcast_select_fusion.2), channel_id=1, source_target_pairs={{8,0},{16,8},{24,16},{9,1},{17,9},{25,17},{10,2},{18,10},{26,18},{... | collective-permute-start | bytes 786440 | tf_op jit(solution)/shard_map/while/body/eval_jaxpr/ppermute | solution.py:15
  127.9 0.6 copy-start.6
  127.9 0.8 copy-start.1
  128.5 41.5 %reduce-scatter.8.cloned.1.call-start = ((), (), s32[]{:S(2)}) async-start(), calls=%async_computation.5 | async-start | bytes 786432 | tf_op jit(solution)/shard_map/while/body/eval_jaxpr/reduce_scatter | solution.py:104
  171.3 17.3 %copy-start.7 = (bf16[128,16]{0,1:T(8,128)(2,1)S(1)}, bf16[128,16]{0,1:T(8,128)(2,1)}, u32[]{:S(2)}) copy-start(bf16[128,16]{0,1:T(8,128)(2,1)} %get-tuple-element.472) | copy-start | bytes 12292 | tf_op jit(solution)/shard_map/while
  171.3 29.5 %copy-start.3 = (bf16[128,2048]{1,0:T(8,128)(2,1)S(1)}, bf16[128,2048]{1,0:T(8,128)(2,1)}, u32[]{:S(2)}) copy-start(bf16[128,2048]{1,0:T(8,128)(2,1)} %get-tuple-element.471) | copy-start | bytes 1572868 | tf_op jit(solution)/shard_map/while
  171.3 47.0 %copy-start.5 = (bf16[2048,16]{0,1:T(8,128)(2,1)S(1)}, bf16[2048,16]{0,1:T(8,128)(2,1)}, u32[]{:S(2)}) copy-start(bf16[2048,16]{0,1:T(8,128)(2,1)} %get-tuple-element.470) | copy-start | bytes 196612 | tf_op jit(solution)/shard_map/while
  171.3 29.5 %reduce-scatter.6.cloned.1.call-start = ((), (), s32[]{:S(2)}) async-start(), calls=%async_computation.4 | async-start | bytes 12288 | tf_op jit(solution)/shard_map/while/body/eval_jaxpr/reduce_scatter | solution.py:107
  171.4 3.6 %collective-permute-start = (bf16[64,2048]{1,0:T(8,128)(2,1)S(1)}, bf16[64,2048]{1,0:T(8,128)(2,1)S(1)}, u32[]{:S(2)}, u32[]{:S(2)}) collective-permute-start(bf16[64,2048]{1,0:T(8,128)(2,1)S(1)} %broadcast_select_fusion.2), channel_id=1, source_target_pairs={{8,0},{16,8},{24,16},{9,1},{17,9},{25,17},{10,2},{18,10},{26,18},{... | collective-permute-start | bytes 786440 | tf_op jit(solution)/shard_map/while/body/eval_jaxpr/ppermute | solution.py:15
  176.0 11.0 %copy-start.4 = (bf16[16,2048]{1,0:T(8,128)(2,1)S(1)}, bf16[16,2048]{1,0:T(8,128)(2,1)}, u32[]{:S(2)}) copy-start(bf16[16,2048]{1,0:T(8,128)(2,1)} %get-tuple-element.221) | copy-start | bytes 196612 | tf_op jit(solution)/shard_map/while/body/eval_jaxpr/cond
  187.2 0.6 copy-start.6
  187.2 0.8 copy-start.1
  187.9 30.4 %reduce-scatter.8.cloned.1.call-start = ((), (), s32[]{:S(2)}) async-start(), calls=%async_computation.5 | async-start | bytes 786432 | tf_op jit(solution)/shard_map/while/body/eval_jaxpr/reduce_scatter | solution.py:104
  219.5 17.2 %copy-start.7 = (bf16[128,16]{0,1:T(8,128)(2,1)S(1)}, bf16[128,16]{0,1:T(8,128)(2,1)}, u32[]{:S(2)}) copy-start(bf16[128,16]{0,1:T(8,128)(2,1)} %get-tuple-element.472) | copy-start | bytes 12292 | tf_op jit(solution)/shard_map/while
  219.6 25.7 %copy-start.3 = (bf16[128,2048]{1,0:T(8,128)(2,1)S(1)}, bf16[128,2048]{1,0:T(8,128)(2,1)}, u32[]{:S(2)}) copy-start(bf16[128,2048]{1,0:T(8,128)(2,1)} %get-tuple-element.471) | copy-start | bytes 1572868 | tf_op jit(solution)/shard_map/while
  219.6 43.1 %copy-start.5 = (bf16[2048,16]{0,1:T(8,128)(2,1)S(1)}, bf16[2048,16]{0,1:T(8,128)(2,1)}, u32[]{:S(2)}) copy-start(bf16[2048,16]{0,1:T(8,128)(2,1)} %get-tuple-element.470) | copy-start | bytes 196612 | tf_op jit(solution)/shard_map/while
  219.6 25.7 %reduce-scatter.6.cloned.1.call-start = ((), (), s32[]{:S(2)}) async-start(), calls=%async_computation.4 | async-start | bytes 12288 | tf_op jit(solution)/shard_map/while/body/eval_jaxpr/reduce_scatter | solution.py:107
  219.7 3.6 %collective-permute-start = (bf16[64,2048]{1,0:T(8,128)(2,1)S(1)}, bf16[64,2048]{1,0:T(8,128)(2,1)S(1)}, u32[]{:S(2)}, u32[]{:S(2)}) collective-permute-start(bf16[64,2048]{1,0:T(8,128)(2,1)S(1)} %broadcast_select_fusion.2), channel_id=1, source_target_pairs={{8,0},{16,8},{24,16},{9,1},{17,9},{25,17},{10,2},{18,10},{26,18},{... | collective-permute-start | bytes 786440 | tf_op jit(solution)/shard_map/while/body/eval_jaxpr/ppermute | solution.py:15
  224.3 11.0 %copy-start.4 = (bf16[16,2048]{1,0:T(8,128)(2,1)S(1)}, bf16[16,2048]{1,0:T(8,128)(2,1)}, u32[]{:S(2)}) copy-start(bf16[16,2048]{1,0:T(8,128)(2,1)} %get-tuple-element.221) | copy-start | bytes 196612 | tf_op jit(solution)/shard_map/while/body/eval_jaxpr/cond
  235.5 0.6 copy-start.6
  235.5 0.8 copy-start.1
  236.1 26.5 %reduce-scatter.8.cloned.1.call-start = ((), (), s32[]{:S(2)}) async-start(), calls=%async_computation.5 | async-start | bytes 786432 | tf_op jit(solution)/shard_map/while/body/eval_jaxpr/reduce_scatter | solution.py:104
  263.9 23.6 %copy-start.2 = (bf16[128,2048]{1,0:T(8,128)(2,1)}, bf16[128,2048]{1,0:T(8,128)(2,1)S(1)}, u32[]{:S(2)}) copy-start(bf16[128,2048]{1,0:T(8,128)(2,1)S(1)} %get-tuple-element.244) | copy-start | bytes 1572868
  263.9 22.2 %reduce-scatter.4.cloned.1.call-start = ((), (), s32[]{:S(2)}) async-start(), calls=%async_computation.3 | async-start | bytes 163840 | tf_op jit(solution)/shard_map/reduce_scatter | solution.py:142
Sparse Core Ops, SparseCore 0:
  34.0 22.6 reduce-scatter.5
  59.5 14.6 reduce-scatter.7
  81.0 23.4 reduce-scatter.5
  107.1 14.6 reduce-scatter.7
  128.7 23.9 reduce-scatter.5
  155.3 14.6 reduce-scatter.7
  188.0 12.7 reduce-scatter.5
  203.6 14.6 reduce-scatter.7
  236.2 9.0 reduce-scatter.5
  248.0 14.6 reduce-scatter.7
Sparse Core Ops, SparseCore 1:
  266.6 19.4 reduce-scatter.3
where the time goes:
time: 296 us; the launch traced here: 295 us
  waiting for transfers between devices  205 us (69%)
  matrix products  34.9 us (12%)
  blocking collectives  17.6 us (6%)
  between operations  15.5 us (5%)
  other arithmetic  9.05 us (3%)
  starting transfers between devices  7.58 us (3%)
  local copies, waits for them, and re-layouts  4.08 us (1%)
    reduce_scatter x5, waiting for transfers between devices, section_step(): lax.psum_scatter(inner_tiles.astype(jnp.bfloat16), 'tensor', scatter_dime...  88.1 us
    reduce_scatter x5, waiting for transfers between devices, section_step(): lax.psum_scatter(frozen_part.astype(jnp.bfloat16), 'tensor', scatter_dime...  82.7 us
    dot_general x2, matrix products, local_terms(): lax.dot_general(branch_block, frozen_local, contract_last, preferred_elem...  21.9 us
    reduce_scatter x1, waiting for transfers between devices, shards(): lax.psum_scatter(adapter_local.astype(jnp.bfloat16), 'dp', scatter_dimens...  21.3 us
    all_gather x1, blocking collectives, shards(): shard_piece = lax.all_gather(passage_embedded, 'dp', axis=0, tiled=True)  17.6 us
    ppermute x5, waiting for transfers between devices, shifted(): lax.ppermute(value, axis, [(source, source + steps) for source in range(f...  10.6 us
    ppermute x5, starting transfers between devices, shifted(): lax.ppermute(value, axis, [(source, source + steps) for source in range(f...  7.12 us
    dot_general x5, matrix products, section_step(): jnp.dot(inner_rows_block, down_shard.T, preferred_element_type=jnp.float32)  6.24 us
  transfers between devices with their start and end apart: 16, of which 16 were waited for; matrix products, arithmetic and copies ran while one was open for 2% of the time, Pallas kernels for 0%

commit v1 on v0

v1 whole, which is shorter than its diff:
```python
import functools
import math

import jax
import jax.numpy as jnp
from jax import lax
from jax.experimental import pallas as pl
from jax.experimental.pallas import tpu as pltpu
from jax.sharding import PartitionSpec as P

ADAPTER_SCALE = 2.0
LOSS_SCALE = 32.0
VMEM_GRANT = 8 << 20
COVER_FLOPS = 10_000_000_000
AXES = ("section", "dp", "tensor")
CONTRACT_LAST = (((1,), (1,)), ((), ()))
CONTRACT_FIRST = (((0,), (0,)), ((), ()))


def vmem_call(kernel, outs, inputs, name, flops, smem=(), scratch=()):
    moved = sum(math.prod(v.shape) * v.dtype.itemsize for v in (*inputs, *outs))
    return pl.pallas_call(
        kernel,
        out_shape=outs,
        in_specs=[
            pl.BlockSpec(memory_space=pltpu.SMEM if i in smem else pltpu.VMEM)
            for i in range(len(inputs))
        ],
        out_specs=tuple(pl.BlockSpec(memory_space=pltpu.VMEM) for _ in outs),
        scratch_shapes=list(scratch),
        name=name,
        compiler_params=pltpu.CompilerParams(vmem_limit_bytes=VMEM_GRANT),
        cost_estimate=pl.CostEstimate(flops=flops, bytes_accessed=moved, transcendentals=0),
    )(*inputs)


def exchange(value, partner, sizes):
    sections, replicas, tensors = sizes
    flat = lambda s, d, t: (s * replicas + d) * tensors + t
    pairs = [
        (flat(s, d, t), flat(*partner(s, d, t)))
        for s in range(sections)
        for d in range(replicas)
        for t in range(tensors)
    ]
    return lax.ppermute(value, AXES, pairs)


def split_pairing(active, step):
    def partner(s, d, t):
        if s == active:
            return (s, d, t ^ step)
        if s == active ^ 1:
            return (s, d ^ 1, t)
        return (s ^ 1, d, t)

    return partner


def hop_pairing(upper):
    lower = upper - 1

    def partner(s, d, t):
        if upper % 2:
            return (s ^ 1, d, t)
        if s in (upper, lower):
            return (upper + lower - s, d, t)
        return (s, d ^ 1, t)

    return partner


def gather_pairing(step):
    def partner(s, d, t):
        if s % 2:
            return (s, d ^ step, t)
        return (s ^ 2, d, t)

    return partner


def branch_terms(gradient, slope_ref, up_ref, h_ref, inner_ref):
    h = (gradient * slope_ref[...].astype(jnp.float32)).astype(jnp.bfloat16)
    h_ref[...] = h
    inner_ref[...] = lax.dot_general(
        up_ref[...], h, CONTRACT_LAST, preferred_element_type=jnp.float32
    ).astype(jnp.bfloat16)


def setup_kernel(count, *refs):
    sources = refs[:count]
    scale_ref, at_ref = refs[count : count + 2]
    targets = refs[count + 2 : 2 * count]
    positives_ref, counts_ref, semaphores = refs[2 * count :]
    copies = [
        pltpu.make_async_copy(source, target, semaphores.at[i])
        for i, (source, target) in enumerate(zip(sources, (positives_ref, counts_ref, *targets)))
    ]
    for copy in copies:
        copy.start()
    copies[0].wait()
    copies[1].wait()
    queries = counts_ref.shape[0]
    length = scale_ref.shape[0] // queries
    position = lax.broadcasted_iota(jnp.int32, (length, scale_ref.shape[1]), 0)
    row = lax.broadcasted_iota(jnp.int32, at_ref.shape, 0)
    positive = jnp.zeros(at_ref.shape, jnp.int32)
    for i in range(queries):
        live = counts_ref[i]
        scale_ref[i * length : (i + 1) * length, :] = jnp.where(
            position < live, LOSS_SCALE, 0.0
        ) / live.astype(jnp.float32)
        positive = jnp.where(row == i, positives_ref[i], positive)
    at_ref[...] = positive
    for copy in copies[2:]:
        copy.wait()


def setup(arrays, rows):
    positives, counts, *held = arrays
    outs = [
        jax.ShapeDtypeStruct((rows, 128), jnp.float32),
        jax.ShapeDtypeStruct((counts.shape[0], 128), jnp.int32),
        *(jax.ShapeDtypeStruct(v.shape, v.dtype) for v in held),
    ]
    return pl.pallas_call(
        functools.partial(setup_kernel, len(arrays)),
        out_shape=outs,
        in_specs=[pl.BlockSpec(memory_space=pltpu.HBM) for _ in arrays],
        out_specs=[pl.BlockSpec(memory_space=pltpu.VMEM) for _ in outs],
        scratch_shapes=[
            pltpu.SMEM(positives.shape, positives.dtype),
            pltpu.SMEM(counts.shape, counts.dtype),
            pltpu.SemaphoreType.DMA((len(arrays),)),
        ],
        name="setup",
        compiler_params=pltpu.CompilerParams(vmem_limit_bytes=VMEM_GRANT),
        cost_estimate=pl.CostEstimate(
            flops=COVER_FLOPS, bytes_accessed=1 << 20, transcendentals=0
        ),
    )(*arrays)


def top_kernel(piece_count, bases, scale_ref, at_ref, query_ref, *refs):
    pieces = refs[:piece_count]
    slope_ref, up_ref, top_ref, h_ref, inner_ref, passages_ref = refs[piece_count:]
    queries, width = query_ref.shape
    rows, local = slope_ref.shape
    length = rows // queries
    inverse_root = 1.0 / math.sqrt(width)
    start = pl.multiple_of(lax.axis_index("tensor") * local, local)
    per_piece = pieces[0].shape[0]
    pitch = passages_ref.shape[0] // piece_count
    if pitch > per_piece:
        passages_ref[...] = jnp.zeros_like(passages_ref)
    for k, piece in enumerate(pieces):
        passages_ref[k * pitch : k * pitch + per_piece, :] = piece[...]
    column = lax.broadcasted_iota(jnp.int32, (queries, pitch), 1)
    positive = at_ref[:, :1]
    replica = lax.axis_index("dp")
    scores = lax.dot_general(
        query_ref[...], passages_ref[...], CONTRACT_LAST, preferred_element_type=jnp.float32
    ) * inverse_root
    targets = []
    for base in bases:
        first = 0 if base is None else (replica ^ base) * per_piece
        hit = (positive == column + first) & (column < per_piece)
        targets.append(hit.astype(jnp.float32))
    target = jnp.concatenate(targets, axis=1)
    score_grad = (jax.nn.sigmoid(scores) - target).astype(jnp.bfloat16)
    total = jnp.dot(
        score_grad, passages_ref[:, pl.ds(start, local)], preferred_element_type=jnp.float32
    )
    query_grad = total * inverse_root
    for i in range(queries):
        at = slice(i * length, (i + 1) * length)
        top_ref[at, :] = (query_grad[i : i + 1, :] * scale_ref[at, :1]).astype(jnp.bfloat16)
    branch_terms(top_ref[...].astype(jnp.float32), slope_ref, up_ref, h_ref, inner_ref)


def product_columns(h_ref, weight_ref, first, out_ref):
    width = out_ref.shape[1]
    tile = min(512, width)

    @pl.loop(0, width // tile)
    def _(n):
        at = pl.multiple_of(n * tile, tile)
        rows = pl.ds(pl.multiple_of(first + at, tile), tile)
        out_ref[:, pl.ds(at, tile)] = lax.dot_general(
            h_ref[...], weight_ref[rows, :], CONTRACT_LAST, preferred_element_type=jnp.float32
        ).astype(jnp.bfloat16)


def cross_columns(h_ref, weight_ref, out_refs):
    for step, out_ref in enumerate(out_refs, 1):
        other = lax.axis_index("tensor") ^ step
        product_columns(h_ref, weight_ref, other * out_ref.shape[1], out_ref)


def first_cross_kernel(active, h_ref, weight_ref, *out_refs):
    @pl.when(lax.axis_index("section") == active)
    def _():
        cross_columns(h_ref, weight_ref, out_refs)


def cross_kernel(active, g_ref, slope_ref, up_ref, h_in, inner_in, weight_ref, h_ref, inner_ref, *out_refs):
    is_active = lax.axis_index("section") == active

    @pl.when(is_active)
    def _():
        branch_terms(g_ref[...].astype(jnp.float32), slope_ref, up_ref, h_ref, inner_ref)
        cross_columns(h_ref, weight_ref, out_refs)

    @pl.when(jnp.logical_not(is_active))
    def _():
        h_ref[...] = h_in[...]
        inner_ref[...] = inner_in[...]


def own_kernel(active, h_ref, weight_ref, out_ref):
    @pl.when(lax.axis_index("section") == active)
    def _():
        product_columns(
            h_ref, weight_ref, lax.axis_index("tensor") * out_ref.shape[1], out_ref
        )


def combine_kernel(active, count, *refs):
    g_ref, own_ref, down_ref = refs[:3]
    inner_refs = refs[3 : 3 + count]
    cross_refs = refs[3 + count : 2 + 2 * count]
    kept_refs = refs[2 + 2 * count : -1]
    out_ref = refs[-1]
    is_active = lax.axis_index("section") == active

    for kept_ref in kept_refs:

        @pl.when(jnp.logical_not(is_active))
        def _():
            out_ref[...] = kept_ref[...]

    @pl.when(is_active)
    def _():
        inner = sum(ref[...].astype(jnp.float32) for ref in inner_refs).astype(jnp.bfloat16)
        width = out_ref.shape[1]
        tile = min(512, width)
        for at in range(0, width, tile):
            columns = slice(at, at + tile)
            value = g_ref[:, columns].astype(jnp.float32) + own_ref[:, columns].astype(jnp.float32)
            for ref in cross_refs:
                value = value + ref[:, columns].astype(jnp.float32)
            value = value + ADAPTER_SCALE * lax.dot_general(
                inner,
                down_ref[:, columns],
                CONTRACT_FIRST,
                preferred_element_type=jnp.float32,
            )
            out_ref[:, columns] = value.astype(jnp.bfloat16)


def split_rows(total, keep, keep_ref, send_ref):
    half = keep_ref.shape[0]
    first, second = total[:half, :], total[half:, :]
    keep_ref[...] = jnp.where(keep == 0, first, second)
    send_ref[...] = jnp.where(keep == 0, second, first).astype(send_ref.dtype)


def adapter_kernel(factor, count, replicas, *refs):
    h_ref, stored_ref, saved_ref = refs[:3]
    inner_refs = refs[3 : 3 + count]
    out_refs = refs[3 + count :]
    inner = sum(ref[...].astype(jnp.float32) for ref in inner_refs).astype(jnp.bfloat16)
    down = factor * jnp.dot(inner, stored_ref[...], preferred_element_type=jnp.float32)
    up = factor * jnp.dot(saved_ref[...], h_ref[...], preferred_element_type=jnp.float32)
    total = jnp.concatenate([down, up], axis=0)
    if len(out_refs) == 2:
        split_rows(total, lax.axis_index("dp") // (replicas // 2), *out_refs)
    else:
        out_refs[0][...] = total.astype(jnp.bfloat16)


def fold_kernel(step, kept_ref, received_ref, keep_ref, send_ref):
    total = kept_ref[...] + received_ref[...].astype(jnp.float32)
    split_rows(total, (lax.axis_index("dp") // step) % 2, keep_ref, send_ref)


def shards(
    query_embedded,
    passage_embedded,
    positives,
    counts,
    stored_inputs,
    adapter_inner,
    branch_slope,
    frozen_projection,
    adapter_down,
    adapter_up,
):
    sizes = tuple(lax.axis_size(name) for name in AXES)
    section_count, replica_total, tensor_count = sizes
    few_replicas = replica_total <= 4
    down, up = adapter_down[0].T, adapter_up[0]
    stored, saved, slope = stored_inputs[0], adapter_inner[0].T, branch_slope[0]
    rows, local = slope.shape
    rank = up.shape[0]
    block = jax.ShapeDtypeStruct((rows, local), jnp.bfloat16)
    inner_shape = jax.ShapeDtypeStruct((rank, rows), jnp.bfloat16)

    if few_replicas:
        bases = list(range(replica_total))
        pieces = [passage_embedded] + [
            exchange(passage_embedded, gather_pairing(step), sizes) for step in bases[1:]
        ]
    else:
        bases = [None]
        pieces = [lax.all_gather(passage_embedded, "dp", axis=0, tiled=True)]
    pitch = -(-pieces[0].shape[0] // 16) * 16
    weight = frozen_projection[0]
    scale, at, query_held, pieces[0], slope, up = setup(
        (positives, counts, query_embedded, pieces[0], slope, up), rows
    )
    g, h, inner = vmem_call(
        functools.partial(top_kernel, len(pieces), bases),
        (block, block, inner_shape),
        (scale, at, query_held, *pieces, slope, up),
        "top",
        2 * rows * local * rank,
        scratch=[pltpu.VMEM((len(pieces) * pitch, passage_embedded.shape[1]), jnp.bfloat16)],
    )
    result = None
    for active in range(section_count - 1, -1, -1):
        first = active == section_count - 1
        flops = 2 * rows * local * local * (tensor_count - 1)
        if first:
            crosses = vmem_call(
                functools.partial(first_cross_kernel, active),
                (block,) * (tensor_count - 1),
                (h, weight),
                f"cross{active}",
                flops,
            )
        else:
            h, inner, *crosses = vmem_call(
                functools.partial(cross_kernel, active),
                (block, inner_shape) + (block,) * (tensor_count - 1),
                (g, slope, up, h, inner, weight),
                f"cross{active}",
                flops,
            )
        received = [
            exchange(cross, split_pairing(active, j), sizes) for j, cross in enumerate(crosses, 1)
        ]
        inner_others = [
            exchange(inner, lambda s, d, t, j=j: (s, d, t ^ j), sizes)
            for j in range(1, tensor_count)
        ]
        (own,) = vmem_call(
            functools.partial(own_kernel, active),
            (block,),
            (h, weight),
            f"own{active}",
            2 * rows * local * local,
        )
        inputs = [g, own, down, inner, *inner_others, *received]
        if result is not None:
            inputs.append(result)
        (result,) = vmem_call(
            functools.partial(combine_kernel, active, tensor_count),
            (block,),
            inputs,
            f"combine{active}",
            2 * rows * local * rank,
        )
        if active:
            g = exchange(result, hop_pairing(active), sizes)

    factor = ADAPTER_SCALE / (query_embedded.shape[0] * replica_total)
    halves = lambda n: (
        jax.ShapeDtypeStruct((n, local), jnp.float32),
        jax.ShapeDtypeStruct((n, local), jnp.bfloat16),
    )
    sums = vmem_call(
        functools.partial(adapter_kernel, factor, tensor_count, replica_total),
        halves(rank) if few_replicas else halves(2 * rank)[1:],
        (h, stored, saved, inner, *inner_others),
        "adapter",
        4 * rows * local * rank,
    )
    if few_replicas:
        kept, sent = sums
        step = replica_total // 2
        while True:
            received = exchange(sent, lambda s, d, t, j=step: (s, d ^ j, t), sizes)
            if step == 1:
                break
            step //= 2
            kept, sent = vmem_call(
                functools.partial(fold_kernel, step),
                halves(kept.shape[0] // 2),
                (kept, received),
                f"fold{step}",
                0,
            )
        reduced = kept + received.astype(jnp.float32)
    else:
        reduced = lax.psum_scatter(sums[0], "dp", scatter_dimension=0, tiled=True).astype(
            jnp.float32
        )
    return (result[None], reduced[None])


def solution(mesh):
    return jax.shard_map(
        shards,
        mesh=mesh,
        in_specs=(
            P("dp", None),
            P("dp", None),
            P("dp"),
            P("dp"),
            P("section", "dp", "tensor"),
            P("section", "dp", None),
            P("section", "dp", "tensor"),
            P("section", None, "tensor"),
            P("section", "tensor", None),
            P("section", None, "tensor"),
        ),
        out_specs=(P("section", "dp", "tensor"), P("section", "dp", "tensor")),
        check_vma=False,
    )
```

time: 296 us -> 85.6 us (0.29)
  waiting for transfers between devices: 205 us -> 25.7 us
  matrix products: 34.9 us -> 0 us
  starting transfers between devices: 7.58 us -> 39 us
  blocking collectives: 17.6 us -> 0 us
  between operations: 15.5 us -> 0.76 us
  Pallas kernels: 0 us -> 10.1 us
  other arithmetic: 9.05 us -> 0.64 us
  local copies, waits for them, and re-layouts: 4.08 us -> 9.03 us
    reduce_scatter x11 -> x0, waiting for transfers between devices: 192 us -> none  [the longest x5 88.1 us: section_step(): lax.psum_scatter(inner_tiles.astype(jnp.bfloat16), 'tensor', scatter_dime...]
    dot_general x20 -> x0, matrix products: 34.9 us -> none  [the longest x2 21.9 us: local_terms(): lax.dot_general(branch_block, frozen_local, contract_last, preferred_elem...]
    ppermute x5 -> x16, starting transfers between devices: 7.12 us -> 39 us  [exchange(): return lax.ppermute(value, AXES, pairs)]
    all_gather x1 -> x0, blocking collectives: 17.6 us -> none  [shards(): shard_piece = lax.all_gather(passage_embedded, 'dp', axis=0, tiled=True)]
    ppermute x5 -> x16, waiting for transfers between devices: 10.6 us -> 25.7 us  [exchange(): return lax.ppermute(value, AXES, pairs)]
    pallas_call x0 -> x16, Pallas kernels: none -> 10.1 us  [the longest x15 9.47 us: vmem_call(): pl.pallas_call(kernel, out_shape=outs, in_specs=[pl.BlockSpec(memory_spac...]
    unnamed x5 -> x20, local copies, waits for them, and re-layouts: 0.11 us -> 9.03 us
    convert_element_type x7 -> x0, other arithmetic: 6.14 us -> none  [the longest x5 5.24 us: section_step(): branch_block = (gradient_block.astype(jnp.float32) * slope_block.astype(j...]
  transfers between devices with their start and end apart: 16 -> 16, of which waited for: 16 -> 9; matrix products, arithmetic and copies ran while one was open for 2% -> 1% of each run, Pallas kernels for 0% -> 5%
where the time goes in v1:
time: 85.6 us; the launch traced here: 85.2 us
  starting transfers between devices  39 us (46%)
  waiting for transfers between devices  25.7 us (30%)
  Pallas kernels  10.1 us (12%)
  local copies, waits for them, and re-layouts  9.03 us (11%)
    ppermute x16, starting transfers between devices, exchange(): return lax.ppermute(value, AXES, pairs)  39 us
    ppermute x16, waiting for transfers between devices, exchange(): return lax.ppermute(value, AXES, pairs)  25.7 us
    pallas_call x15, Pallas kernels, vmem_call(): pl.pallas_call(kernel, out_shape=outs, in_specs=[pl.BlockSpec(memory_spac...  9.47 us
    unnamed x20, local copies, waits for them, and re-layouts  9.03 us
  transfers between devices with their start and end apart: 16, of which 9 were waited for; matrix products, arithmetic and copies ran while one was open for 1% of the time, Pallas kernels for 5%

profile of v1, /device:TPU:0, one launch (start us, length us, event | category | flops | bytes accessed | tf_op | source)
XLA Modules:
  0.0 85.2 jit_solution(992335509197526873)
XLA Ops:
  0.6 3.1 %collective-permute-start = (bf16[12,4096]{1,0:T(8,128)(2,1)}, bf16[12,4096]{1,0:T(8,128)(2,1)S(1)}, u32[]{:S(2)}, u32[]{:S(2)}) collective-permute-start(bf16[12,4096]{1,0:T(8,128)(2,1)} %refs_3_.1), channel_id=1, source_target_pairs={{0,16},{1,17},{2,18},{3,19},{4,20},{5,21},{6,22},{7,23},{8,10},{9,... | collective-permute-start | bytes 294920 | tf_op jit(solution)/shard_map/ppermute | solution.py:46
  3.7 0.1 collective-permute-start.1
  3.8 1.9 %collective-permute-start.2 = (bf16[12,4096]{1,0:T(8,128)(2,1)}, bf16[12,4096]{1,0:T(8,128)(2,1)S(1)}, u32[]{:S(2)}, u32[]{:S(2)}) collective-permute-start(bf16[12,4096]{1,0:T(8,128)(2,1)} %refs_3_.1), channel_id=1, source_target_pairs={{0,16},{1,17},{2,18},{3,19},{4,20},{5,21},{6,22},{7,23},{8,14},{9,... | collective-permute-start | bytes 294920 | tf_op jit(solution)/shard_map/ppermute | solution.py:46
  5.7 1.0 %copy-done.4 = bf16[1,128,2048]{2,1,0:T(8,128)(2,1)S(1)} copy-done((bf16[1,128,2048]{2,1,0:T(8,128)(2,1)S(1)}, bf16[1,128,2048]{2,1,0:T(8,128)(2,1)}, u32[]{:S(2)}) %copy-start.4) | copy-done | bytes 524312
  6.8 0.9 %copy-done.5 = bf16[12,4096]{1,0:T(8,128)(2,1)S(1)} copy-done((bf16[12,4096]{1,0:T(8,128)(2,1)S(1)}, bf16[12,4096]{1,0:T(8,128)(2,1)}, u32[]{:S(2)}) %copy-start.5) | copy-done | bytes 98328
  7.7 0.8 copy-done.6
  8.5 0.8 copy-done.7
  9.3 0.7 copy-done.8
  9.9 0.7 copy-done.9
  10.6 0.6 setup.1
  11.2 0.0 collective-permute-done.refs_1_
  11.2 0.0 collective-permute-done.1.refs_2_
  11.2 0.0 collective-permute-done.2.refs_3_
  11.2 0.9 %top.1 = (bf16[128,2048]{1,0:T(8,128)(2,1)S(1)}, bf16[128,2048]{1,0:T(8,128)(2,1)S(1)}, bf16[16,128]{1,0:T(8,128)(2,1)S(1)}) custom-call(f32[128,128]{1,0:T(8,128)S(1)} %get-tuple-element.24.scale_ref, s32[4,128]{1,0:T(4,128)S(1)} %get-tuple-element.25.at_ref, bf16[4,4096]{1,0:T(4,128)(2,1)S(1)} %get-tuple-element.26.query_ref, ...), custom_call_target="tpu_custom_call" | custom-call | flops 8388608 | bytes 2136064 | tf_op jit(solution)/shard_map/top/pallas_call | solution.py:22
  12.2 4.2 %copy-done = bf16[1,4096,2048]{2,1,0:T(8,128)(2,1)S(1)} copy-done((bf16[1,4096,2048]{2,1,0:T(8,128)(2,1)S(1)}, bf16[1,4096,2048]{2,1,0:T(8,128)(2,1)}, u32[]{:S(2)}) %copy-start) | copy-done | bytes 16777240
  16.3 0.0 collective-permute-start.4
  16.4 1.5 %collective-permute-start.3 = (bf16[16,128]{1,0:T(8,128)(2,1)S(1)}, bf16[16,128]{1,0:T(8,128)(2,1)S(1)}, u32[]{:S(2)}, u32[]{:S(2)}) collective-permute-start(bf16[16,128]{1,0:T(8,128)(2,1)S(1)} %get-tuple-element.32.refs_3_.inner_in), channel_id=1, source_target_pairs={{0,1},{1,0},{2,3},{3,2},{4,5},{5,4},{6,7},{7,6},{8,9},{9,8},{10,11... | collective-permute-start | bytes 12296 | tf_op jit(solution)/shard_map/ppermute | solution.py:46
  17.8 2.1 %collective-permute-done.3.refs_4_ = bf16[16,128]{1,0:T(8,128)(2,1)S(1)} collective-permute-done((bf16[16,128]{1,0:T(8,128)(2,1)S(1)}, bf16[16,128]{1,0:T(8,128)(2,1)S(1)}, u32[]{:S(2)}, u32[]{:S(2)}) %collective-permute-start.3) | collective-permute-done | bytes 4128 | tf_op jit(solution)/shard_map/ppermute | solution.py:46
  20.0 0.0 collective-permute-done.4.refs_5_
  20.0 0.0 copy-done.1
  20.0 0.0 collective-permute-start.5
  20.0 1.9 %collective-permute-done.5.g_ref.refs_0_ = bf16[128,2048]{1,0:T(8,128)(2,1)S(1)} collective-permute-done((bf16[128,2048]{1,0:T(8,128)(2,1)S(1)}, bf16[128,2048]{1,0:T(8,128)(2,1)S(1)}, u32[]{:S(2)}, u32[]{:S(2)}) %collective-permute-start.5) | collective-permute-done | bytes 524320 | tf_op jit(solution)/shard_map/ppermute | solution.py:46
  21.9 0.2 collective-permute-start.7
  22.1 1.5 %collective-permute-start.6 = (bf16[16,128]{1,0:T(8,128)(2,1)S(1)}, bf16[16,128]{1,0:T(8,128)(2,1)S(1)}, u32[]{:S(2)}, u32[]{:S(2)}) collective-permute-start(bf16[16,128]{1,0:T(8,128)(2,1)S(1)} %get-tuple-element.34.refs_3_.inner_in), channel_id=1, source_target_pairs={{0,1},{1,0},{2,3},{3,2},{4,5},{5,4},{6,7},{7,6},{8,9},{9,8},{10,11... | collective-permute-start | bytes 12296 | tf_op jit(solution)/shard_map/ppermute | solution.py:46
  23.6 2.1 %collective-permute-done.6.refs_4_ = bf16[16,128]{1,0:T(8,128)(2,1)S(1)} collective-permute-done((bf16[16,128]{1,0:T(8,128)(2,1)S(1)}, bf16[16,128]{1,0:T(8,128)(2,1)S(1)}, u32[]{:S(2)}, u32[]{:S(2)}) %collective-permute-start.6) | collective-permute-done | bytes 4128 | tf_op jit(solution)/shard_map/ppermute | solution.py:46
  25.7 0.0 collective-permute-done.7.refs_5_
  25.8 1.6 %collective-permute-start.8 = (bf16[128,2048]{1,0:T(8,128)(2,1)S(1)}, bf16[128,2048]{1,0:T(8,128)(2,1)S(1)}, u32[]{:S(2)}, u32[]{:S(2)}) collective-permute-start(bf16[128,2048]{1,0:T(8,128)(2,1)S(1)} %combine2.1.refs_6_), channel_id=1, source_target_pairs={{0,2},{1,3},{2,0},{3,1},{4,6},{5,7},{6,4},{7,5},{8,16},{9,17},{10,... | collective-permute-start | bytes 1572872 | tf_op jit(solution)/shard_map/ppermute | solution.py:46
  27.4 7.6 %collective-permute-done.8.g_ref.refs_0_ = bf16[128,2048]{1,0:T(8,128)(2,1)S(1)} collective-permute-done((bf16[128,2048]{1,0:T(8,128)(2,1)S(1)}, bf16[128,2048]{1,0:T(8,128)(2,1)S(1)}, u32[]{:S(2)}, u32[]{:S(2)}) %collective-permute-start.8) | collective-permute-done | bytes 524320 | tf_op jit(solution)/shard_map/ppermute | solution.py:46
  35.1 1.6 %collective-permute-start.10 = (bf16[128,2048]{1,0:T(8,128)(2,1)S(1)}, bf16[128,2048]{1,0:T(8,128)(2,1)S(1)}, u32[]{:S(2)}, u32[]{:S(2)}) collective-permute-start(bf16[128,2048]{1,0:T(8,128)(2,1)S(1)} %get-tuple-element.38), channel_id=1, source_target_pairs={{0,2},{1,3},{2,0},{3,1},{4,6},{5,7},{6,4},{7,5},{8,9},{9,8},{10,11... | collective-permute-start | bytes 1572872 | tf_op jit(solution)/shard_map/ppermute | solution.py:46
  36.7 1.5 %collective-permute-start.9 = (bf16[16,128]{1,0:T(8,128)(2,1)S(1)}, bf16[16,128]{1,0:T(8,128)(2,1)S(1)}, u32[]{:S(2)}, u32[]{:S(2)}) collective-permute-start(bf16[16,128]{1,0:T(8,128)(2,1)S(1)} %get-tuple-element.37.refs_3_.inner_in), channel_id=1, source_target_pairs={{0,1},{1,0},{2,3},{3,2},{4,5},{5,4},{6,7},{7,6},{8,9},{9,8},{10,11... | collective-permute-start | bytes 12296 | tf_op jit(solution)/shard_map/ppermute | solution.py:46
  38.2 2.1 %collective-permute-done.9.refs_4_ = bf16[16,128]{1,0:T(8,128)(2,1)S(1)} collective-permute-done((bf16[16,128]{1,0:T(8,128)(2,1)S(1)}, bf16[16,128]{1,0:T(8,128)(2,1)S(1)}, u32[]{:S(2)}, u32[]{:S(2)}) %collective-permute-start.9) | collective-permute-done | bytes 4128 | tf_op jit(solution)/shard_map/ppermute | solution.py:46
  40.3 4.0 %collective-permute-done.10.refs_5_ = bf16[128,2048]{1,0:T(8,128)(2,1)S(1)} collective-permute-done((bf16[128,2048]{1,0:T(8,128)(2,1)S(1)}, bf16[128,2048]{1,0:T(8,128)(2,1)S(1)}, u32[]{:S(2)}, u32[]{:S(2)}) %collective-permute-start.10) | collective-permute-done | bytes 524320 | tf_op jit(solution)/shard_map/ppermute | solution.py:46
  44.4 19.4 %collective-permute-start.11 = (bf16[128,2048]{1,0:T(8,128)(2,1)S(1)}, bf16[128,2048]{1,0:T(8,128)(2,1)S(1)}, u32[]{:S(2)}, u32[]{:S(2)}) collective-permute-start(bf16[128,2048]{1,0:T(8,128)(2,1)S(1)} %combine1.1.refs_6_), channel_id=1, source_target_pairs={{0,8},{1,9},{2,10},{3,11},{4,12},{5,13},{6,14},{7,15},{8,0},{9,1},... | collective-permute-start | bytes 1572872 | tf_op jit(solution)/shard_map/ppermute | solution.py:46
  63.8 1.5 %collective-permute-done.11.g_ref.refs_0_ = bf16[128,2048]{1,0:T(8,128)(2,1)S(1)} collective-permute-done((bf16[128,2048]{1,0:T(8,128)(2,1)S(1)}, bf16[128,2048]{1,0:T(8,128)(2,1)S(1)}, u32[]{:S(2)}, u32[]{:S(2)}) %collective-permute-start.11) | collective-permute-done | bytes 524320 | tf_op jit(solution)/shard_map/ppermute | solution.py:46
  65.3 3.6 %cross0.1 = (bf16[128,2048]{1,0:T(8,128)(2,1)S(1)}, bf16[16,128]{1,0:T(8,128)(2,1)S(1)}, bf16[128,2048]{1,0:T(8,128)(2,1)S(1)}) custom-call(bf16[128,2048]{1,0:T(8,128)(2,1)S(1)} %collective-permute-done.11.g_ref.refs_0_, bf16[128,2048]{1,0:T(8,128)(2,1)S(1)} %get-tuple-element.28.refs_4_.slope_ref, bf16[16,2048]{1,0:T(8,128)(2,1)S(1)} %get-tuple-element.29.refs_5_.up_ref, ...), custom_call_target="tpu_custom_call" | custom-call | flops 1073741824 | bytes 19472384 | tf_op jit(solution)/shard_map/cross0/pallas_call | solution.py:22
  68.9 1.5 %collective-permute-start.12 = (bf16[16,128]{1,0:T(8,128)(2,1)S(1)}, bf16[16,128]{1,0:T(8,128)(2,1)S(1)}, u32[]{:S(2)}, u32[]{:S(2)}) collective-permute-start(bf16[16,128]{1,0:T(8,128)(2,1)S(1)} %get-tuple-element.40.refs_3_), channel_id=1, source_target_pairs={{0,1},{1,0},{2,3},{3,2},{4,5},{5,4},{6,7},{7,6},{8,9},{9,8},{10,11... | collective-permute-start | bytes 12296 | tf_op jit(solution)/shard_map/ppermute | solution.py:46
  70.5 2.1 %collective-permute-done.12.refs_4_ = bf16[16,128]{1,0:T(8,128)(2,1)S(1)} collective-permute-done((bf16[16,128]{1,0:T(8,128)(2,1)S(1)}, bf16[16,128]{1,0:T(8,128)(2,1)S(1)}, u32[]{:S(2)}, u32[]{:S(2)}) %collective-permute-start.12) | collective-permute-done | bytes 4128 | tf_op jit(solution)/shard_map/ppermute | solution.py:46
  72.6 0.0 copy-done.2
  72.6 0.2 adapter.1
  72.9 1.7 %collective-permute-start.14 = (bf16[16,2048]{1,0:T(8,128)(2,1)S(1)}, bf16[16,2048]{1,0:T(8,128)(2,1)S(1)}, u32[]{:S(2)}, u32[]{:S(2)}) collective-permute-start(bf16[16,2048]{1,0:T(8,128)(2,1)S(1)} %get-tuple-element.43), channel_id=1, source_target_pairs={{0,4},{1,5},{2,6},{3,7},{4,0},{5,1},{6,2},{7,3},{8,12},{9,13},{10,... | collective-permute-start | bytes 196616 | tf_op jit(solution)/shard_map/ppermute | solution.py:46
  74.5 1.5 %collective-permute-start.13 = (bf16[128,2048]{1,0:T(8,128)(2,1)S(1)}, bf16[128,2048]{1,0:T(8,128)(2,1)S(1)}, u32[]{:S(2)}, u32[]{:S(2)}) collective-permute-start(bf16[128,2048]{1,0:T(8,128)(2,1)S(1)} %get-tuple-element.41), channel_id=1, source_target_pairs={{0,1},{1,0},{2,3},{3,2},{4,5},{5,4},{6,7},{7,6},{8,10},{9,11},{10,... | collective-permute-start | bytes 1572872 | tf_op jit(solution)/shard_map/ppermute | solution.py:46
  76.1 2.1 %collective-permute-done.14.received_ref = bf16[16,2048]{1,0:T(8,128)(2,1)S(1)} collective-permute-done((bf16[16,2048]{1,0:T(8,128)(2,1)S(1)}, bf16[16,2048]{1,0:T(8,128)(2,1)S(1)}, u32[]{:S(2)}, u32[]{:S(2)}) %collective-permute-start.14) | collective-permute-done | bytes 65568 | tf_op jit(solution)/shard_map/ppermute | solution.py:46
  78.2 1.8 %collective-permute-start.15 = (bf16[8,2048]{1,0:T(8,128)(2,1)S(1)}, bf16[8,2048]{1,0:T(8,128)(2,1)S(1)}, u32[]{:S(2)}, u32[]{:S(2)}) collective-permute-start(bf16[8,2048]{1,0:T(8,128)(2,1)S(1)} %get-tuple-element.45), channel_id=1, source_target_pairs={{0,2},{1,3},{2,0},{3,1},{4,6},{5,7},{6,4},{7,5},{8,10},{9,11},{10,... | collective-permute-start | bytes 98312 | tf_op jit(solution)/shard_map/ppermute | solution.py:46
  80.1 3.3 %own0.1.refs_1_ = bf16[128,2048]{1,0:T(8,128)(2,1)S(1)} custom-call(bf16[128,2048]{1,0:T(8,128)(2,1)S(1)} %get-tuple-element.39.h_ref.refs_0_, bf16[4096,2048]{1,0:T(8,128)(2,1)S(1)} %bitcast.20), custom_call_target="tpu_custom_call" | custom-call | flops 1073741824 | bytes 17825792 | tf_op jit(solution)/shard_map/own0/pallas_call | solution.py:22
  83.4 0.0 collective-permute-done.15
  83.4 0.6 add_bitcast_fusion
  84.1 0.0 collective-permute-done.13.refs_5_
  84.1 1.2 %combine0.1 = bf16[128,2048]{1,0:T(8,128)(2,1)} custom-call(bf16[128,2048]{1,0:T(8,128)(2,1)S(1)} %collective-permute-done.11.g_ref.refs_0_, bf16[128,2048]{1,0:T(8,128)(2,1)S(1)} %own0.1.refs_1_, bf16[16,2048]{1,0:T(8,128)(2,1)S(1)} %bitcast.24, bf16[16,128]{1,0:T(8,128)(2,1)S(1)} %get-tuple-element.40.refs_3_, ...), custom_call_target="tpu_custom_call" | custom-call | flops 8388608 | bytes 2695168 | tf_op jit(solution)/shard_map/combine0/pallas_call | solution.py:22
  (21 shorter events, 0.2 us)
Async XLA Ops:
  0.6 10.6 %collective-permute-start = (bf16[12,4096]{1,0:T(8,128)(2,1)}, bf16[12,4096]{1,0:T(8,128)(2,1)S(1)}, u32[]{:S(2)}, u32[]{:S(2)}) collective-permute-start(bf16[12,4096]{1,0:T(8,128)(2,1)} %refs_3_.1), channel_id=1, source_target_pairs={{0,16},{1,17},{2,18},{3,19},{4,20},{5,21},{6,22},{7,23},{8,10},{9,... | collective-permute-start | bytes 294920 | tf_op jit(solution)/shard_map/ppermute | solution.py:46
  3.7 7.5 %collective-permute-start.1 = (bf16[12,4096]{1,0:T(8,128)(2,1)}, bf16[12,4096]{1,0:T(8,128)(2,1)S(1)}, u32[]{:S(2)}, u32[]{:S(2)}) collective-permute-start(bf16[12,4096]{1,0:T(8,128)(2,1)} %refs_3_.1), channel_id=1, source_target_pairs={{0,16},{1,17},{2,18},{3,19},{4,20},{5,21},{6,22},{7,23},{8,12},{9,... | collective-permute-start | bytes 294920 | tf_op jit(solution)/shard_map/ppermute | solution.py:46
  3.8 7.5 %collective-permute-start.2 = (bf16[12,4096]{1,0:T(8,128)(2,1)}, bf16[12,4096]{1,0:T(8,128)(2,1)S(1)}, u32[]{:S(2)}, u32[]{:S(2)}) collective-permute-start(bf16[12,4096]{1,0:T(8,128)(2,1)} %refs_3_.1), channel_id=1, source_target_pairs={{0,16},{1,17},{2,18},{3,19},{4,20},{5,21},{6,22},{7,23},{8,14},{9,... | collective-permute-start | bytes 294920 | tf_op jit(solution)/shard_map/ppermute | solution.py:46
  5.7 1.0 %copy-start.4 = (bf16[1,128,2048]{2,1,0:T(8,128)(2,1)S(1)}, bf16[1,128,2048]{2,1,0:T(8,128)(2,1)}, u32[]{:S(2)}) copy-start(bf16[1,128,2048]{2,1,0:T(8,128)(2,1)} %param.16) | copy-start | bytes 1572868
  6.8 0.9 %copy-start.5 = (bf16[12,4096]{1,0:T(8,128)(2,1)S(1)}, bf16[12,4096]{1,0:T(8,128)(2,1)}, u32[]{:S(2)}) copy-start(bf16[12,4096]{1,0:T(8,128)(2,1)} %refs_3_.1) | copy-start | bytes 294916
  7.7 0.8 copy-start.6
  8.5 0.8 copy-start.7
  9.3 0.7 copy-start.8
  9.9 0.7 copy-start.9
  10.6 5.8 %copy-start = (bf16[1,4096,2048]{2,1,0:T(8,128)(2,1)S(1)}, bf16[1,4096,2048]{2,1,0:T(8,128)(2,1)}, u32[]{:S(2)}) copy-start(bf16[1,4096,2048]{2,1,0:T(8,128)(2,1)} %param.17) | copy-start | bytes 50331652
  16.3 3.6 %copy-start.1 = (bf16[1,2048,16]{1,2,0:T(8,128)(2,1)S(1)}, bf16[1,2048,16]{1,2,0:T(8,128)(2,1)}, u32[]{:S(2)}) copy-start(bf16[1,2048,16]{1,2,0:T(8,128)(2,1)} %param.18) | copy-start | bytes 196612
  16.3 3.6 %collective-permute-start.4 = (bf16[128,2048]{1,0:T(8,128)(2,1)S(1)}, bf16[128,2048]{1,0:T(8,128)(2,1)S(1)}, u32[]{:S(2)}, u32[]{:S(2)}) collective-permute-start(bf16[128,2048]{1,0:T(8,128)(2,1)S(1)} %cross3.1), channel_id=1, source_target_pairs={{0,8},{1,9},{2,10},{3,11},{4,12},{5,13},{6,14},{7,15},{8,0},{9,1},... | collective-permute-start | bytes 1572872 | tf_op jit(solution)/shard_map/ppermute | solution.py:46
  16.4 3.6 %collective-permute-start.3 = (bf16[16,128]{1,0:T(8,128)(2,1)S(1)}, bf16[16,128]{1,0:T(8,128)(2,1)S(1)}, u32[]{:S(2)}, u32[]{:S(2)}) collective-permute-start(bf16[16,128]{1,0:T(8,128)(2,1)S(1)} %get-tuple-element.32.refs_3_.inner_in), channel_id=1, source_target_pairs={{0,1},{1,0},{2,3},{3,2},{4,5},{5,4},{6,7},{7,6},{8,9},{9,8},{10,11... | collective-permute-start | bytes 12296 | tf_op jit(solution)/shard_map/ppermute | solution.py:46
  20.0 1.9 %collective-permute-start.5 = (bf16[128,2048]{1,0:T(8,128)(2,1)S(1)}, bf16[128,2048]{1,0:T(8,128)(2,1)S(1)}, u32[]{:S(2)}, u32[]{:S(2)}) collective-permute-start(bf16[128,2048]{1,0:T(8,128)(2,1)S(1)} %combine3.1.refs_6_), channel_id=1, source_target_pairs={{0,8},{1,9},{2,10},{3,11},{4,12},{5,13},{6,14},{7,15},{8,0},{9,1},... | collective-permute-start | bytes 1572872 | tf_op jit(solution)/shard_map/ppermute | solution.py:46
  21.9 3.8 %collective-permute-start.7 = (bf16[128,2048]{1,0:T(8,128)(2,1)S(1)}, bf16[128,2048]{1,0:T(8,128)(2,1)S(1)}, u32[]{:S(2)}, u32[]{:S(2)}) collective-permute-start(bf16[128,2048]{1,0:T(8,128)(2,1)S(1)} %get-tuple-element.35), channel_id=1, source_target_pairs={{0,8},{1,9},{2,10},{3,11},{4,12},{5,13},{6,14},{7,15},{8,0},{9,1},... | collective-permute-start | bytes 1572872 | tf_op jit(solution)/shard_map/ppermute | solution.py:46
  22.1 3.6 %collective-permute-start.6 = (bf16[16,128]{1,0:T(8,128)(2,1)S(1)}, bf16[16,128]{1,0:T(8,128)(2,1)S(1)}, u32[]{:S(2)}, u32[]{:S(2)}) collective-permute-start(bf16[16,128]{1,0:T(8,128)(2,1)S(1)} %get-tuple-element.34.refs_3_.inner_in), channel_id=1, source_target_pairs={{0,1},{1,0},{2,3},{3,2},{4,5},{5,4},{6,7},{7,6},{8,9},{9,8},{10,11... | collective-permute-start | bytes 12296 | tf_op jit(solution)/shard_map/ppermute | solution.py:46
  25.8 9.2 %collective-permute-start.8 = (bf16[128,2048]{1,0:T(8,128)(2,1)S(1)}, bf16[128,2048]{1,0:T(8,128)(2,1)S(1)}, u32[]{:S(2)}, u32[]{:S(2)}) collective-permute-start(bf16[128,2048]{1,0:T(8,128)(2,1)S(1)} %combine2.1.refs_6_), channel_id=1, source_target_pairs={{0,2},{1,3},{2,0},{3,1},{4,6},{5,7},{6,4},{7,5},{8,16},{9,17},{10,... | collective-permute-start | bytes 1572872 | tf_op jit(solution)/shard_map/ppermute | solution.py:46
  35.1 9.2 %collective-permute-start.10 = (bf16[128,2048]{1,0:T(8,128)(2,1)S(1)}, bf16[128,2048]{1,0:T(8,128)(2,1)S(1)}, u32[]{:S(2)}, u32[]{:S(2)}) collective-permute-start(bf16[128,2048]{1,0:T(8,128)(2,1)S(1)} %get-tuple-element.38), channel_id=1, source_target_pairs={{0,2},{1,3},{2,0},{3,1},{4,6},{5,7},{6,4},{7,5},{8,9},{9,8},{10,11... | collective-permute-start | bytes 1572872 | tf_op jit(solution)/shard_map/ppermute | solution.py:46
  36.7 3.6 %collective-permute-start.9 = (bf16[16,128]{1,0:T(8,128)(2,1)S(1)}, bf16[16,128]{1,0:T(8,128)(2,1)S(1)}, u32[]{:S(2)}, u32[]{:S(2)}) collective-permute-start(bf16[16,128]{1,0:T(8,128)(2,1)S(1)} %get-tuple-element.37.refs_3_.inner_in), channel_id=1, source_target_pairs={{0,1},{1,0},{2,3},{3,2},{4,5},{5,4},{6,7},{7,6},{8,9},{9,8},{10,11... | collective-permute-start | bytes 12296 | tf_op jit(solution)/shard_map/ppermute | solution.py:46
  38.2 34.4 %copy-start.2 = (bf16[1,128,2048]{2,1,0:T(8,128)(2,1)S(1)}, bf16[1,128,2048]{2,1,0:T(8,128)(2,1)}, u32[]{:S(2)}) copy-start(bf16[1,128,2048]{2,1,0:T(8,128)(2,1)} %param.14) | copy-start | bytes 1572868
  38.2 34.4 %copy-start.3 = (bf16[1,128,16]{1,2,0:T(8,128)(2,1)S(1)}, bf16[1,128,16]{1,2,0:T(8,128)(2,1)}, u32[]{:S(2)}) copy-start(bf16[1,128,16]{1,2,0:T(8,128)(2,1)} %param.15) | copy-start | bytes 12292
  44.4 21.0 %collective-permute-start.11 = (bf16[128,2048]{1,0:T(8,128)(2,1)S(1)}, bf16[128,2048]{1,0:T(8,128)(2,1)S(1)}, u32[]{:S(2)}, u32[]{:S(2)}) collective-permute-start(bf16[128,2048]{1,0:T(8,128)(2,1)S(1)} %combine1.1.refs_6_), channel_id=1, source_target_pairs={{0,8},{1,9},{2,10},{3,11},{4,12},{5,13},{6,14},{7,15},{8,0},{9,1},... | collective-permute-start | bytes 1572872 | tf_op jit(solution)/shard_map/ppermute | solution.py:46
  68.9 3.7 %collective-permute-start.12 = (bf16[16,128]{1,0:T(8,128)(2,1)S(1)}, bf16[16,128]{1,0:T(8,128)(2,1)S(1)}, u32[]{:S(2)}, u32[]{:S(2)}) collective-permute-start(bf16[16,128]{1,0:T(8,128)(2,1)S(1)} %get-tuple-element.40.refs_3_), channel_id=1, source_target_pairs={{0,1},{1,0},{2,3},{3,2},{4,5},{5,4},{6,7},{7,6},{8,9},{9,8},{10,11... | collective-permute-start | bytes 12296 | tf_op jit(solution)/shard_map/ppermute | solution.py:46
  72.9 5.3 %collective-permute-start.14 = (bf16[16,2048]{1,0:T(8,128)(2,1)S(1)}, bf16[16,2048]{1,0:T(8,128)(2,1)S(1)}, u32[]{:S(2)}, u32[]{:S(2)}) collective-permute-start(bf16[16,2048]{1,0:T(8,128)(2,1)S(1)} %get-tuple-element.43), channel_id=1, source_target_pairs={{0,4},{1,5},{2,6},{3,7},{4,0},{5,1},{6,2},{7,3},{8,12},{9,13},{10,... | collective-permute-start | bytes 196616 | tf_op jit(solution)/shard_map/ppermute | solution.py:46
  74.5 9.5 %collective-permute-start.13 = (bf16[128,2048]{1,0:T(8,128)(2,1)S(1)}, bf16[128,2048]{1,0:T(8,128)(2,1)S(1)}, u32[]{:S(2)}, u32[]{:S(2)}) collective-permute-start(bf16[128,2048]{1,0:T(8,128)(2,1)S(1)} %get-tuple-element.41), channel_id=1, source_target_pairs={{0,1},{1,0},{2,3},{3,2},{4,5},{5,4},{6,7},{7,6},{8,10},{9,11},{10,... | collective-permute-start | bytes 1572872 | tf_op jit(solution)/shard_map/ppermute | solution.py:46
  78.2 5.2 %collective-permute-start.15 = (bf16[8,2048]{1,0:T(8,128)(2,1)S(1)}, bf16[8,2048]{1,0:T(8,128)(2,1)S(1)}, u32[]{:S(2)}, u32[]{:S(2)}) collective-permute-start(bf16[8,2048]{1,0:T(8,128)(2,1)S(1)} %get-tuple-element.45), channel_id=1, source_target_pairs={{0,2},{1,3},{2,0},{3,1},{4,6},{5,7},{6,4},{7,5},{8,10},{9,11},{10,... | collective-permute-start | bytes 98312 | tf_op jit(solution)/shard_map/ppermute | solution.py:46

commit v2 on v1

v2 whole, which is shorter than its diff:
```python
import functools
import math

import jax
import jax.numpy as jnp
from jax import lax
from jax.experimental import pallas as pl
from jax.experimental.pallas import tpu as pltpu
from jax.sharding import PartitionSpec as P


ADAPTER_SCALE = 2.0
LOSS_SCALE = 32.0
VMEM_GRANT = 8 << 20
COVER_FLOPS = 10_000_000_000
CHUNKS = 2
MATMUL_TILE = 1024
AXES = ("section", "dp", "tensor")
CONTRACT_LAST = (((1,), (1,)), ((), ()))
CONTRACT_FIRST = (((0,), (0,)), ((), ()))


def vmem_call(kernel, outs, inputs, flops, smem=(), scratch=()):
    moved = sum(math.prod(v.shape) * v.dtype.itemsize for v in (*inputs, *outs))
    return pl.pallas_call(
        kernel,
        out_shape=outs,
        in_specs=[
            pl.BlockSpec(memory_space=pltpu.SMEM if i in smem else pltpu.VMEM)
            for i in range(len(inputs))
        ],
        out_specs=tuple(pl.BlockSpec(memory_space=pltpu.VMEM) for _ in outs),
        scratch_shapes=list(scratch),
        compiler_params=pltpu.CompilerParams(vmem_limit_bytes=VMEM_GRANT),
        cost_estimate=pl.CostEstimate(flops=flops, bytes_accessed=moved, transcendentals=0),
    )(*inputs)


def exchange(value, partner, sizes):
    sections, replicas, tensors = sizes
    flat = lambda s, d, t: (s * replicas + d) * tensors + t
    pairs = [
        (flat(s, d, t), flat(*partner(s, d, t)))
        for s in range(sections)
        for d in range(replicas)
        for t in range(tensors)
    ]
    return lax.ppermute(value, AXES, pairs)


def split_pairing(active, step):
    def partner(s, d, t):
        if s == active:
            return (s, d, t ^ step)
        if s == active ^ 1:
            return (s, d ^ 1, t)
        return (s ^ 1, d, t)

    return partner


def hop_pairing(upper):
    lower = upper - 1

    def partner(s, d, t):
        if upper % 2:
            return (s ^ 1, d, t)
        if s in (upper, lower):
            return (upper + lower - s, d, t)
        return (s, d ^ 1, t)

    return partner


def gather_pairing(step):
    def partner(s, d, t):
        if s % 2:
            return (s, d ^ step, t)
        return (s ^ 2, d, t)

    return partner


def branch(g_ref, slope_ref, chunk):
    width = g_ref.shape[1]
    slope = slope_ref[:, chunk * width : (chunk + 1) * width].astype(jnp.float32)
    return (g_ref[...].astype(jnp.float32) * slope).astype(jnp.bfloat16)


def inner_terms(h_refs, up_ref):
    total = 0.0
    for k, h_ref in enumerate(h_refs):
        width = h_ref.shape[1]
        total = total + lax.dot_general(
            up_ref[:, k * width : (k + 1) * width],
            h_ref[...],
            CONTRACT_LAST,
            preferred_element_type=jnp.float32,
        )
    return total.astype(jnp.bfloat16)


def pack_inner(inner_ref, out_ref, rows):
    if out_ref.shape[0] > rows:
        tail = jnp.zeros((out_ref.shape[0] - rows, out_ref.shape[1] - rows), out_ref.dtype)
        out_ref[rows:, :] = jnp.concatenate([inner_ref[...], tail], axis=1)


def unpack_inner(ref, rows):
    return ref[...] if ref.shape[0] < rows else ref[rows:, :rows]


def products(h_refs, parts, weight_ref, first, out_ref, base_ref=None, base_at=0):
    width = out_ref.shape[1]
    tile = min(MATMUL_TILE, width)
    for at in range(0, width, tile):
        rows = pl.ds(pl.multiple_of(first + at, tile), tile)
        total = 0.0
        if base_ref is not None:
            total = base_ref[:, base_at + at : base_at + at + tile]
        for h_ref, part in zip(h_refs, parts):
            depth = h_ref.shape[1]
            total = total + lax.dot_general(
                h_ref[...],
                weight_ref[rows, part * depth : (part + 1) * depth],
                CONTRACT_LAST,
                preferred_element_type=jnp.float32,
            )
        out_ref[: total.shape[0], at : at + tile] = total.astype(out_ref.dtype)


def setup_kernel(count, *refs):
    sources = refs[:count]
    scale_ref, at_ref = refs[count : count + 2]
    targets = refs[count + 2 : 2 * count]
    positives_ref, counts_ref, semaphores = refs[2 * count :]
    copies = [
        pltpu.make_async_copy(source, target, semaphores.at[i])
        for i, (source, target) in enumerate(zip(sources, (positives_ref, counts_ref, *targets)))
    ]
    for copy in copies:
        copy.start()
    copies[0].wait()
    copies[1].wait()
    queries = counts_ref.shape[0]
    length = scale_ref.shape[0] // queries
    position = lax.broadcasted_iota(jnp.int32, (length, scale_ref.shape[1]), 0)
    row = lax.broadcasted_iota(jnp.int32, at_ref.shape, 0)
    positive = jnp.zeros(at_ref.shape, jnp.int32)
    for i in range(queries):
        live = counts_ref[i]
        scale_ref[i * length : (i + 1) * length, :] = jnp.where(
            position < live, LOSS_SCALE, 0.0
        ) / live.astype(jnp.float32)
        positive = jnp.where(row == i, positives_ref[i], positive)
    at_ref[...] = positive
    for copy in copies[2:]:
        copy.wait()


def setup(arrays, rows):
    positives, counts, *held = arrays
    outs = [
        jax.ShapeDtypeStruct((rows, 128), jnp.float32),
        jax.ShapeDtypeStruct((counts.shape[0], 128), jnp.int32),
        *(jax.ShapeDtypeStruct(v.shape, v.dtype) for v in held),
    ]
    return pl.pallas_call(
        functools.partial(setup_kernel, len(arrays)),
        out_shape=outs,
        in_specs=[pl.BlockSpec(memory_space=pltpu.HBM) for _ in arrays],
        out_specs=[pl.BlockSpec(memory_space=pltpu.VMEM) for _ in outs],
        scratch_shapes=[
            pltpu.SMEM(positives.shape, positives.dtype),
            pltpu.SMEM(counts.shape, counts.dtype),
            pltpu.SemaphoreType.DMA((len(arrays),)),
        ],
        name="setup",
        compiler_params=pltpu.CompilerParams(vmem_limit_bytes=VMEM_GRANT),
        cost_estimate=pl.CostEstimate(
            flops=COVER_FLOPS, bytes_accessed=1 << 20, transcendentals=0
        ),
    )(*arrays)


def top_kernel(piece_count, bases, scale_ref, at_ref, query_ref, *refs):
    pieces = refs[:piece_count]
    slope_ref, *out_refs, passages_ref = refs[piece_count:]
    top_refs, h_refs = out_refs[: len(out_refs) // 2], out_refs[len(out_refs) // 2 :]
    queries, width = query_ref.shape
    rows, local = slope_ref.shape
    length = rows // queries
    inverse_root = 1.0 / math.sqrt(width)
    start = pl.multiple_of(lax.axis_index("tensor") * local, local)
    per_piece = pieces[0].shape[0]
    pitch = passages_ref.shape[0] // piece_count
    if pitch > per_piece:
        passages_ref[...] = jnp.zeros_like(passages_ref)
    for k, piece in enumerate(pieces):
        passages_ref[k * pitch : k * pitch + per_piece, :] = piece[...]
    column = lax.broadcasted_iota(jnp.int32, (queries, pitch), 1)
    positive = at_ref[:, :1]
    replica = lax.axis_index("dp")
    scores = lax.dot_general(
        query_ref[...], passages_ref[...], CONTRACT_LAST, preferred_element_type=jnp.float32
    ) * inverse_root
    targets = []
    for base in bases:
        first = 0 if base is None else (replica ^ base) * per_piece
        hit = (positive == column + first) & (column < per_piece)
        targets.append(hit.astype(jnp.float32))
    target = jnp.concatenate(targets, axis=1)
    score_grad = (jax.nn.sigmoid(scores) - target).astype(jnp.bfloat16)
    total = jnp.dot(
        score_grad, passages_ref[:, pl.ds(start, local)], preferred_element_type=jnp.float32
    )
    query_grad = total * inverse_root
    for i in range(queries):
        at = slice(i * length, (i + 1) * length)
        block = (query_grad[i : i + 1, :] * scale_ref[at, :1]).astype(jnp.bfloat16)
        for k, top_ref in enumerate(top_refs):
            width = top_ref.shape[1]
            top_ref[at, :] = block[:, k * width : (k + 1) * width]
    for k, (top_ref, h_ref) in enumerate(zip(top_refs, h_refs)):
        h_ref[...] = branch(top_ref, slope_ref, k)


def when_section(active, then, otherwise=None):
    is_active = lax.axis_index("section") == active
    pl.when(is_active)(then)
    if otherwise is not None:
        pl.when(jnp.logical_not(is_active))(otherwise)


def early_kernel(active, g_ref, slope_ref, h_in, weight_ref, h_ref, *base_refs):
    def run():
        h_ref[...] = branch(g_ref, slope_ref, 0)
        for step, base_ref in enumerate(base_refs, 1):
            other = lax.axis_index("tensor") ^ step
            products([h_ref], [0], weight_ref, other * base_ref.shape[1], base_ref)

    def keep():
        h_ref[...] = h_in[...]

    when_section(active, run, keep)


def first_cross_kernel(active, count, offset, local, up_ref, weight_ref, *refs):
    h_refs, (inner_ref, *out_refs) = refs[:count], refs[count:]

    def run():
        for step, out_ref in enumerate(out_refs, 1):
            other = lax.axis_index("tensor") ^ step
            products(h_refs, range(count), weight_ref, other * local + offset, out_ref)
            pack_inner(inner_ref, out_ref, h_refs[0].shape[0])

    inner_ref[...] = inner_terms(h_refs, up_ref)
    when_section(active, run)


def next_cross_kernel(active, count, g_ref, slope_ref, up_ref, h_in, inner_in, weight_ref, *refs):
    first_h, *base_refs = refs[:count]
    h_ref, inner_ref, *out_refs = refs[count:]

    def run():
        h_ref[...] = branch(g_ref, slope_ref, 1)
        inner_ref[...] = inner_terms([first_h, h_ref], up_ref)
        for step, (base_ref, out_ref) in enumerate(zip(base_refs, out_refs), 1):
            other = lax.axis_index("tensor") ^ step
            products([h_ref], [1], weight_ref, other * base_ref.shape[1], out_ref, base_ref)
            pack_inner(inner_ref, out_ref, h_ref.shape[0])

    def keep():
        h_ref[...] = h_in[...]
        inner_ref[...] = inner_in[...]

    when_section(active, run, keep)


def later_cross_kernel(active, count, parts, offset, local, after_ref, weight_ref, *refs):
    del after_ref
    h_refs, rest = refs[: len(parts)], refs[len(parts) :]
    out_refs = rest[-count:]
    base_refs = rest[:-count] or [None] * count

    def run():
        for step, (base_ref, out_ref) in enumerate(zip(base_refs, out_refs), 1):
            other = lax.axis_index("tensor") ^ step
            products(
                h_refs, parts, weight_ref, other * local + offset, out_ref, base_ref, offset
            )

    when_section(active, run)


def own_kernel(active, offset, local, weight_ref, *refs):
    *h_refs, out_ref = refs

    def run():
        first = lax.axis_index("tensor") * local + offset
        products(h_refs, range(len(h_refs)), weight_ref, first, out_ref)

    when_section(active, run)


def combine_kernel(active, offset, count, chunks, *refs):
    g_refs, refs = refs[:chunks], refs[chunks:]
    own_ref, down_ref = refs[:2]
    inner_refs = refs[2 : 2 + count]
    cross_refs = refs[2 + count : 1 + 2 * count]
    kept_refs, out_ref = refs[1 + 2 * count : -1], refs[-1]
    rows = out_ref.shape[0]

    def run():
        inner = sum(unpack_inner(ref, rows).astype(jnp.float32) for ref in inner_refs)
        inner = inner.astype(jnp.bfloat16)
        width = g_refs[0].shape[1]
        for k, g_ref in enumerate(g_refs):
            at = slice(k * width, (k + 1) * width)
            value = g_ref[...].astype(jnp.float32) + own_ref[:, at].astype(jnp.float32)
            for ref in cross_refs:
                value = value + ref[:rows, at].astype(jnp.float32)
            value = value + ADAPTER_SCALE * lax.dot_general(
                inner,
                down_ref[:, offset + k * width : offset + (k + 1) * width],
                CONTRACT_FIRST,
                preferred_element_type=jnp.float32,
            )
            out_ref[:, at] = value.astype(jnp.bfloat16)

    def keep():
        for k, kept_ref in enumerate(kept_refs):
            width = kept_ref.shape[1]
            out_ref[:, k * width : (k + 1) * width] = kept_ref[...]

    when_section(active, run, keep if kept_refs else None)


def split_rows(total, keep, keep_ref, send_ref):
    half = keep_ref.shape[0]
    first, second = total[:half, :], total[half:, :]
    keep_ref[...] = jnp.where(keep == 0, first, second)
    send_ref[...] = jnp.where(keep == 0, second, first).astype(send_ref.dtype)


def adapter_kernel(factor, count, chunks, replicas, *refs):
    stored_ref, saved_ref = refs[:2]
    h_refs = refs[2 : 2 + chunks]
    inner_refs = refs[2 + chunks : 2 + chunks + count]
    out_refs = refs[2 + chunks + count :]
    inner = sum(ref[...].astype(jnp.float32) for ref in inner_refs).astype(jnp.bfloat16)
    down = factor * jnp.dot(inner, stored_ref[...], preferred_element_type=jnp.float32)
    ups = [
        factor * jnp.dot(saved_ref[...], h_ref[...], preferred_element_type=jnp.float32)
        for h_ref in h_refs
    ]
    total = jnp.concatenate([down, jnp.concatenate(ups, axis=1)], axis=0)
    if len(out_refs) == 2:
        split_rows(total, lax.axis_index("dp") // (replicas // 2), *out_refs)
    else:
        out_refs[0][...] = total.astype(jnp.bfloat16)


def fold_kernel(step, kept_ref, received_ref, keep_ref, send_ref):
    total = kept_ref[...] + received_ref[...].astype(jnp.float32)
    split_rows(total, (lax.axis_index("dp") // step) % 2, keep_ref, send_ref)


def shards(
    query_embedded,
    passage_embedded,
    positives,
    counts,
    stored_inputs,
    adapter_inner,
    branch_slope,
    frozen_projection,
    adapter_down,
    adapter_up,
):
    sizes = tuple(lax.axis_size(name) for name in AXES)
    section_count, replica_total, tensor_count = sizes
    few_replicas = replica_total <= 4
    weight, down, up = frozen_projection[0], adapter_down[0].T, adapter_up[0]
    stored, saved, slope = stored_inputs[0], adapter_inner[0].T, branch_slope[0]
    rows, local = slope.shape
    rank = up.shape[0]
    span = local // CHUNKS
    others = range(1, tensor_count)
    struct = lambda n, kind=jnp.bfloat16: jax.ShapeDtypeStruct((rows, n), kind)
    inner_shape = jax.ShapeDtypeStruct((rank, rows), jnp.bfloat16)
    matmul_flops = lambda depth, columns: 2 * rows * depth * columns

    if few_replicas:
        bases = list(range(replica_total))
        pieces = [passage_embedded] + [
            exchange(passage_embedded, gather_pairing(step), sizes)
            for step in bases[1:]
        ]
    else:
        bases = [None]
        pieces = [lax.all_gather(passage_embedded, "dp", axis=0, tiled=True)]
    pitch = -(-pieces[0].shape[0] // 16) * 16
    scale, at, query_held, pieces[0], slope, up = setup(
        (positives, counts, query_embedded, pieces[0], slope, up), rows
    )
    tops = vmem_call(
        functools.partial(top_kernel, len(pieces), bases),
        (struct(span),) * (2 * CHUNKS),
        (scale, at, query_held, *pieces, slope),
        0,
        scratch=[pltpu.VMEM((len(pieces) * pitch, passage_embedded.shape[1]), jnp.bfloat16)],
    )
    g, h = tops[:CHUNKS], tops[CHUNKS:]
    inner = None
    results = None
    for active in range(section_count - 1, -1, -1):
        last = active == 0
        width = local if last else span
        offsets = range(0, local, width)
        received = {}
        payload = jax.ShapeDtypeStruct((rows if last else rows + rank, width), jnp.bfloat16)
        swap = lambda values: [
            exchange(value, split_pairing(active, j), sizes)
            for j, value in zip(others, values)
        ]
        if inner is None:
            inner, *crosses = vmem_call(
                functools.partial(first_cross_kernel, active, CHUNKS, 0, local),
                (inner_shape,) + (payload,) * len(others),
                (up, weight, *h),
                matmul_flops(local, width) * len(others),
            )
            parts, bases_held, cross_h = list(range(CHUNKS)), [], h
        else:
            first_h, *bases_held = vmem_call(
                functools.partial(early_kernel, active),
                (struct(span),) + (struct(local, jnp.float32),) * len(others),
                (g[0], slope, h[0], weight),
                matmul_flops(span, local) * len(others),
            )
            second_h, inner, *crosses = vmem_call(
                functools.partial(next_cross_kernel, active, 1 + len(others)),
                (struct(span), inner_shape) + (payload,) * len(others),
                (g[1], slope, up, h[1], inner, weight, first_h, *bases_held),
                matmul_flops(span, width) * len(others),
            )
            h = [first_h, second_h]
            parts, cross_h = [1], [second_h]
        received[0] = swap(crosses)
        inner_others = received[0]
        if last:
            inner_others = [
                exchange(inner, lambda s, d, t, j=j: (s, d, t ^ j), sizes)
                for j in others
            ]
        for offset in offsets[1:]:
            crosses = vmem_call(
                functools.partial(
                    later_cross_kernel, active, len(others), parts, offset, local
                ),
                (struct(width),) * len(others),
                (crosses[0], weight, *cross_h, *bases_held),
                matmul_flops(span * len(parts), width) * len(others),
            )
            received[offset] = swap(crosses)
        sums, next_g = [], []
        for k, offset in enumerate(offsets):
            (own,) = vmem_call(
                functools.partial(own_kernel, active, offset, local),
                (struct(width),),
                (weight, *h),
                matmul_flops(local, width),
            )
            g_parts = g if last else [g[k]]
            kept = [] if results is None else results if last else [results[k]]
            (total,) = vmem_call(
                functools.partial(
                    combine_kernel, active, offset, tensor_count, len(g_parts)
                ),
                (struct(width),),
                (
                    *g_parts,
                    own,
                    down,
                    inner,
                    *inner_others,
                    *received[offset],
                    *kept,
                ),
                matmul_flops(rank, width),
            )
            sums.append(total)
            if not last:
                next_g.append(exchange(total, hop_pairing(active), sizes))
        results, g = sums, next_g
    result = results[0]

    factor = ADAPTER_SCALE / (query_embedded.shape[0] * replica_total)
    halves = lambda n: (
        jax.ShapeDtypeStruct((n, local), jnp.float32),
        jax.ShapeDtypeStruct((n, local), jnp.bfloat16),
    )
    sums = vmem_call(
        functools.partial(adapter_kernel, factor, tensor_count, CHUNKS, replica_total),
        halves(rank) if few_replicas else halves(2 * rank)[1:],
        (stored, saved, *h, inner, *inner_others),
        4 * rows * local * rank,
    )
    if few_replicas:
        kept, sent = sums
        step = replica_total // 2
        while True:
            received = exchange(sent, lambda s, d, t, j=step: (s, d ^ j, t), sizes)
            if step == 1:
                break
            step //= 2
            kept, sent = vmem_call(
                functools.partial(fold_kernel, step),
                halves(kept.shape[0] // 2),
                (kept, received),
                0,
            )
        reduced = kept + received.astype(jnp.float32)
    else:
        reduced = lax.psum_scatter(sums[0], "dp", scatter_dimension=0, tiled=True).astype(
            jnp.float32
        )
    return (result[None], reduced[None])


def solution(mesh):
    return jax.shard_map(
        shards,
        mesh=mesh,
        in_specs=(
            P("dp", None),
            P("dp", None),
            P("dp"),
            P("dp"),
            P("section", "dp", "tensor"),
            P("section", "dp", None),
            P("section", "dp", "tensor"),
            P("section", None, "tensor"),
            P("section", "tensor", None),
            P("section", None, "tensor"),
        ),
        out_specs=(P("section", "dp", "tensor"), P("section", "dp", "tensor")),
        check_vma=False,
    )
```

time: 85.6 us -> 75.2 us (0.88)
  waiting for transfers between devices: 25.7 us -> 19.6 us
  starting transfers between devices: 39 us -> 35.3 us
  Pallas kernels: 10.1 us -> 9.2 us
    ppermute x16 -> x19, waiting for transfers between devices: 25.7 us -> 19.6 us  [exchange(): return lax.ppermute(value, AXES, pairs)]
    ppermute x16 -> x19, starting transfers between devices: 39 us -> 35.3 us  [exchange(): return lax.ppermute(value, AXES, pairs)]
    pallas_call x15 -> x27, Pallas kernels: 9.47 us -> 8.58 us  [vmem_call(): pl.pallas_call(kernel, out_shape=outs, in_specs=[pl.BlockSpec(memory_spac...]
  transfers between devices with their start and end apart: 16 -> 19, of which waited for: 9 -> 11; matrix products, arithmetic and copies ran while one was open for 1% -> 1% of each run, Pallas kernels for 5% -> 7%
where the time goes in v2:
time: 75.2 us; the launch traced here: 74.8 us
  starting transfers between devices  35.3 us (47%)
  waiting for transfers between devices  19.6 us (26%)
  local copies, waits for them, and re-layouts  9.3 us (12%)
  Pallas kernels  9.2 us (12%)
  between operations  0.83 us (1%)
    ppermute x19, starting transfers between devices, exchange(): return lax.ppermute(value, AXES, pairs)  35.3 us
    ppermute x19, waiting for transfers between devices, exchange(): return lax.ppermute(value, AXES, pairs)  19.6 us
    unnamed x20, local copies, waits for them, and re-layouts  9.3 us
    pallas_call x27, Pallas kernels, vmem_call(): pl.pallas_call(kernel, out_shape=outs, in_specs=[pl.BlockSpec(memory_spac...  8.58 us
  transfers between devices with their start and end apart: 19, of which 11 were waited for; matrix products, arithmetic and copies ran while one was open for 1% of the time, Pallas kernels for 7%

profile of v2, /device:TPU:0, one launch (start us, length us, event | category | flops | bytes accessed | tf_op | source)
XLA Modules:
  0.0 74.8 jit_solution(1624752950619791931)
XLA Ops:
  0.6 3.1 %collective-permute-start = (bf16[12,4096]{1,0:T(8,128)(2,1)}, bf16[12,4096]{1,0:T(8,128)(2,1)S(1)}, u32[]{:S(2)}, u32[]{:S(2)}) collective-permute-start(bf16[12,4096]{1,0:T(8,128)(2,1)} %refs_3_.1), channel_id=1, source_target_pairs={{0,16},{1,17},{2,18},{3,19},{4,20},{5,21},{6,22},{7,23},{8,10},{9,... | collective-permute-start | bytes 294920 | tf_op jit(solution)/shard_map/ppermute | solution.py:48
  3.7 0.1 collective-permute-start.2
  3.8 1.9 %collective-permute-start.1 = (bf16[12,4096]{1,0:T(8,128)(2,1)}, bf16[12,4096]{1,0:T(8,128)(2,1)S(1)}, u32[]{:S(2)}, u32[]{:S(2)}) collective-permute-start(bf16[12,4096]{1,0:T(8,128)(2,1)} %refs_3_.1), channel_id=1, source_target_pairs={{0,16},{1,17},{2,18},{3,19},{4,20},{5,21},{6,22},{7,23},{8,12},{9,... | collective-permute-start | bytes 294920 | tf_op jit(solution)/shard_map/ppermute | solution.py:48
  5.7 1.0 %copy-done.4 = bf16[1,128,2048]{2,1,0:T(8,128)(2,1)S(1)} copy-done((bf16[1,128,2048]{2,1,0:T(8,128)(2,1)S(1)}, bf16[1,128,2048]{2,1,0:T(8,128)(2,1)}, u32[]{:S(2)}) %copy-start.4) | copy-done | bytes 524312
  6.8 0.9 %copy-done.5 = bf16[12,4096]{1,0:T(8,128)(2,1)S(1)} copy-done((bf16[12,4096]{1,0:T(8,128)(2,1)S(1)}, bf16[12,4096]{1,0:T(8,128)(2,1)}, u32[]{:S(2)}) %copy-start.5) | copy-done | bytes 98328
  7.7 0.8 %copy-done.6 = bf16[1,16,2048]{2,1,0:T(8,128)(2,1)S(1)} copy-done((bf16[1,16,2048]{2,1,0:T(8,128)(2,1)S(1)}, bf16[1,16,2048]{2,1,0:T(8,128)(2,1)}, u32[]{:S(2)}) %copy-start.6) | copy-done | bytes 65560
  8.5 0.8 %copy-done.7 = bf16[4,4096]{1,0:T(4,128)(2,1)S(1)} copy-done((bf16[4,4096]{1,0:T(4,128)(2,1)S(1)}, bf16[4,4096]{1,0:T(4,128)(2,1)}, u32[]{:S(2)}) %copy-start.7) | copy-done | bytes 32792
  9.3 0.7 copy-done.8
  9.9 0.7 copy-done.9
  10.6 0.6 setup.1
  11.2 0.0 collective-permute-done.refs_1_
  11.2 0.7 shard_map.113
  11.9 4.4 %copy-done = bf16[1,4096,2048]{2,1,0:T(8,128)(2,1)S(1)} copy-done((bf16[1,4096,2048]{2,1,0:T(8,128)(2,1)S(1)}, bf16[1,4096,2048]{2,1,0:T(8,128)(2,1)}, u32[]{:S(2)}) %copy-start) | copy-done | bytes 16777240
  16.3 0.2 shard_map.115
  16.6 0.5 collective-permute-start.5
  17.1 1.1 %collective-permute-done.3.refs_4_.refs_5_ = bf16[144,1024]{1,0:T(8,128)(2,1)S(1)} collective-permute-done((bf16[144,1024]{1,0:T(8,128)(2,1)S(1)}, bf16[144,1024]{1,0:T(8,128)(2,1)S(1)}, u32[]{:S(2)}, u32[]{:S(2)}) %collective-permute-start.3) | collective-permute-done | bytes 294944 | tf_op jit(solution)/shard_map/ppermute | solution.py:48
  18.2 0.1 collective-permute-start.4
  18.3 0.2 collective-permute-done.5.refs_5_
  18.6 0.1 collective-permute-start.6
  18.7 1.0 %collective-permute-done.4.g_ref.refs_0_ = bf16[128,1024]{1,0:T(8,128)(2,1)S(1)} collective-permute-done((bf16[128,1024]{1,0:T(8,128)(2,1)S(1)}, bf16[128,1024]{1,0:T(8,128)(2,1)S(1)}, u32[]{:S(2)}, u32[]{:S(2)}) %collective-permute-start.4) | collective-permute-done | bytes 262176 | tf_op jit(solution)/shard_map/ppermute | solution.py:48
  19.7 0.4 collective-permute-done.6.g_ref.refs_0_
  20.1 0.2 collective-permute-start.7
  20.3 0.4 collective-permute-start.9
  20.7 1.1 %collective-permute-done.7.refs_4_.refs_5_ = bf16[144,1024]{1,0:T(8,128)(2,1)S(1)} collective-permute-done((bf16[144,1024]{1,0:T(8,128)(2,1)S(1)}, bf16[144,1024]{1,0:T(8,128)(2,1)S(1)}, u32[]{:S(2)}, u32[]{:S(2)}) %collective-permute-start.7) | collective-permute-done | bytes 294944 | tf_op jit(solution)/shard_map/ppermute | solution.py:48
  21.8 1.6 %collective-permute-start.8 = (bf16[128,1024]{1,0:T(8,128)(2,1)S(1)}, bf16[128,1024]{1,0:T(8,128)(2,1)S(1)}, u32[]{:S(2)}, u32[]{:S(2)}) collective-permute-start(bf16[128,1024]{1,0:T(8,128)(2,1)S(1)} %shard_map.123.refs_6_), channel_id=1, source_target_pairs={{0,2},{1,3},{2,0},{3,1},{4,6},{5,7},{6,4},{7,5},{8,16},{9,17},{10,... | collective-permute-start | bytes 786440 | tf_op jit(solution)/shard_map/ppermute | solution.py:48
  23.5 0.5 collective-permute-start.10
  24.0 4.3 %collective-permute-done.8.g_ref.refs_0_ = bf16[128,1024]{1,0:T(8,128)(2,1)S(1)} collective-permute-done((bf16[128,1024]{1,0:T(8,128)(2,1)S(1)}, bf16[128,1024]{1,0:T(8,128)(2,1)S(1)}, u32[]{:S(2)}, u32[]{:S(2)}) %collective-permute-start.8) | collective-permute-done | bytes 262176 | tf_op jit(solution)/shard_map/ppermute | solution.py:48
  28.3 2.8 %collective-permute-done.10.g_ref.refs_0_ = bf16[128,1024]{1,0:T(8,128)(2,1)S(1)} collective-permute-done((bf16[128,1024]{1,0:T(8,128)(2,1)S(1)}, bf16[128,1024]{1,0:T(8,128)(2,1)S(1)}, u32[]{:S(2)}, u32[]{:S(2)}) %collective-permute-start.10) | collective-permute-done | bytes 262176 | tf_op jit(solution)/shard_map/ppermute | solution.py:48
  31.1 1.6 %collective-permute-start.11 = (bf16[144,1024]{1,0:T(8,128)(2,1)S(1)}, bf16[144,1024]{1,0:T(8,128)(2,1)S(1)}, u32[]{:S(2)}, u32[]{:S(2)}) collective-permute-start(bf16[144,1024]{1,0:T(8,128)(2,1)S(1)} %get-tuple-element.54.after_ref), channel_id=1, source_target_pairs={{0,2},{1,3},{2,0},{3,1},{4,6},{5,7},{6,4},{7,5},{8,9},{9,8},{10,11... | collective-permute-start | bytes 884744 | tf_op jit(solution)/shard_map/ppermute | solution.py:48
  32.7 0.4 collective-permute-start.13
  33.2 4.7 %collective-permute-done.11.refs_4_.refs_5_ = bf16[144,1024]{1,0:T(8,128)(2,1)S(1)} collective-permute-done((bf16[144,1024]{1,0:T(8,128)(2,1)S(1)}, bf16[144,1024]{1,0:T(8,128)(2,1)S(1)}, u32[]{:S(2)}, u32[]{:S(2)}) %collective-permute-start.11) | collective-permute-done | bytes 294944 | tf_op jit(solution)/shard_map/ppermute | solution.py:48
  37.9 14.0 %collective-permute-start.12 = (bf16[128,1024]{1,0:T(8,128)(2,1)S(1)}, bf16[128,1024]{1,0:T(8,128)(2,1)S(1)}, u32[]{:S(2)}, u32[]{:S(2)}) collective-permute-start(bf16[128,1024]{1,0:T(8,128)(2,1)S(1)} %shard_map.130.refs_7_), channel_id=1, source_target_pairs={{0,8},{1,9},{2,10},{3,11},{4,12},{5,13},{6,14},{7,15},{8,0},{9,1},... | collective-permute-start | bytes 786440 | tf_op jit(solution)/shard_map/ppermute | solution.py:48
  51.9 0.0 copy-start.2
  51.9 0.0 copy-start.3
  51.9 2.8 %collective-permute-start.14 = (bf16[128,1024]{1,0:T(8,128)(2,1)S(1)}, bf16[128,1024]{1,0:T(8,128)(2,1)S(1)}, u32[]{:S(2)}, u32[]{:S(2)}) collective-permute-start(bf16[128,1024]{1,0:T(8,128)(2,1)S(1)} %shard_map.133.refs_8_), channel_id=1, source_target_pairs={{0,8},{1,9},{2,10},{3,11},{4,12},{5,13},{6,14},{7,15},{8,0},{9,1},... | collective-permute-start | bytes 786440 | tf_op jit(solution)/shard_map/ppermute | solution.py:48
  54.7 1.5 %shard_map.134 = (bf16[128,1024]{1,0:T(8,128)(2,1)S(1)}, f32[128,2048]{1,0:T(8,128)S(1)}) custom-call(bf16[128,1024]{1,0:T(8,128)(2,1)S(1)} %collective-permute-done.12.g_ref.refs_0_, bf16[128,2048]{1,0:T(8,128)(2,1)S(1)} %get-tuple-element.37.refs_4_.slope_ref, bf16[128,1024]{1,0:T(8,128)(2,1)S(1)} %get-tuple-element.50.refs_0_.h_in, ...), custom_call_target="tpu_custom_call" | custom-call | flops 536870912 | bytes 19136512 | tf_op jit(solution)/shard_map/pallas_call | solution.py:25
  56.3 1.7 %shard_map.135 = (bf16[128,1024]{1,0:T(8,128)(2,1)S(1)}, bf16[16,128]{1,0:T(8,128)(2,1)S(1)}, bf16[128,2048]{1,0:T(8,128)(2,1)S(1)}) custom-call(bf16[128,1024]{1,0:T(8,128)(2,1)S(1)} %collective-permute-done.14.g_ref.refs_1_, bf16[128,2048]{1,0:T(8,128)(2,1)S(1)} %get-tuple-element.37.refs_4_.slope_ref, bf16[16,2048]{1,0:T(8,128)(2,1)S(1)} %get-tuple-element.41.up_ref, ...), custom_call_target="tpu_custom_call" | custom-call | flops 536870912 | bytes 19996672 | tf_op jit(solution)/shard_map/pallas_call | solution.py:25
  57.9 1.6 %collective-permute-start.15 = (bf16[16,128]{1,0:T(8,128)(2,1)S(1)}, bf16[16,128]{1,0:T(8,128)(2,1)S(1)}, u32[]{:S(2)}, u32[]{:S(2)}) collective-permute-start(bf16[16,128]{1,0:T(8,128)(2,1)S(1)} %get-tuple-element.58.refs_4_), channel_id=1, source_target_pairs={{0,1},{1,0},{2,3},{3,2},{4,5},{5,4},{6,7},{7,6},{8,9},{9,8},{10,11... | collective-permute-start | bytes 12296 | tf_op jit(solution)/shard_map/ppermute | solution.py:48
  59.5 2.1 %collective-permute-done.15.refs_5_ = bf16[16,128]{1,0:T(8,128)(2,1)S(1)} collective-permute-done((bf16[16,128]{1,0:T(8,128)(2,1)S(1)}, bf16[16,128]{1,0:T(8,128)(2,1)S(1)}, u32[]{:S(2)}, u32[]{:S(2)}) %collective-permute-start.15) | collective-permute-done | bytes 4128 | tf_op jit(solution)/shard_map/ppermute | solution.py:48
  61.6 0.2 shard_map.138
  61.8 2.6 %collective-permute-start.17 = (bf16[16,2048]{1,0:T(8,128)(2,1)S(1)}, bf16[16,2048]{1,0:T(8,128)(2,1)S(1)}, u32[]{:S(2)}, u32[]{:S(2)}) collective-permute-start(bf16[16,2048]{1,0:T(8,128)(2,1)S(1)} %get-tuple-element.61), channel_id=1, source_target_pairs={{0,4},{1,5},{2,6},{3,7},{4,0},{5,1},{6,2},{7,3},{8,12},{9,13},{10,... | collective-permute-start | bytes 196616 | tf_op jit(solution)/shard_map/ppermute | solution.py:48
  64.4 1.5 %collective-permute-start.16 = (bf16[128,2048]{1,0:T(8,128)(2,1)S(1)}, bf16[128,2048]{1,0:T(8,128)(2,1)S(1)}, u32[]{:S(2)}, u32[]{:S(2)}) collective-permute-start(bf16[128,2048]{1,0:T(8,128)(2,1)S(1)} %get-tuple-element.59), channel_id=1, source_target_pairs={{0,1},{1,0},{2,3},{3,2},{4,5},{5,4},{6,7},{7,6},{8,10},{9,11},{10,... | collective-permute-start | bytes 1572872 | tf_op jit(solution)/shard_map/ppermute | solution.py:48
  65.9 1.2 %collective-permute-done.17.received_ref = bf16[16,2048]{1,0:T(8,128)(2,1)S(1)} collective-permute-done((bf16[16,2048]{1,0:T(8,128)(2,1)S(1)}, bf16[16,2048]{1,0:T(8,128)(2,1)S(1)}, u32[]{:S(2)}, u32[]{:S(2)}) %collective-permute-start.17) | collective-permute-done | bytes 65568 | tf_op jit(solution)/shard_map/ppermute | solution.py:48
  67.2 2.2 %collective-permute-start.18 = (bf16[8,2048]{1,0:T(8,128)(2,1)S(1)}, bf16[8,2048]{1,0:T(8,128)(2,1)S(1)}, u32[]{:S(2)}, u32[]{:S(2)}) collective-permute-start(bf16[8,2048]{1,0:T(8,128)(2,1)S(1)} %get-tuple-element.63), channel_id=1, source_target_pairs={{0,2},{1,3},{2,0},{3,1},{4,6},{5,7},{6,4},{7,5},{8,10},{9,11},{10,... | collective-permute-start | bytes 98312 | tf_op jit(solution)/shard_map/ppermute | solution.py:48
  69.4 2.9 %shard_map.136.refs_2_ = bf16[128,2048]{1,0:T(8,128)(2,1)S(1)} custom-call(bf16[4096,2048]{1,0:T(8,128)(2,1)S(1)} %bitcast.29, bf16[128,1024]{1,0:T(8,128)(2,1)S(1)} %get-tuple-element.55.refs_0_.refs_2_, bf16[128,1024]{1,0:T(8,128)(2,1)S(1)} %get-tuple-element.57.refs_1_.refs_3_), custom_call_target="tpu_custom_call" | custom-call | flops 1073741824 | bytes 17825792 | tf_op jit(solution)/shard_map/pallas_call | solution.py:25
  72.3 0.6 add_bitcast_fusion
  72.9 0.7 collective-permute-done.16.refs_6_
  73.6 1.2 %shard_map.137 = bf16[128,2048]{1,0:T(8,128)(2,1)} custom-call(bf16[128,1024]{1,0:T(8,128)(2,1)S(1)} %collective-permute-done.12.g_ref.refs_0_, bf16[128,1024]{1,0:T(8,128)(2,1)S(1)} %collective-permute-done.14.g_ref.refs_1_, bf16[128,2048]{1,0:T(8,128)(2,1)S(1)} %shard_map.136.refs_2_, bf16[16,2048]{1,0:T(8,128)(2,1)S(1)} %bitcast.36, ...), custom_call_target="tpu_custom_call" | custom-call | flops 8388608 | bytes 2695168 | tf_op jit(solution)/shard_map/pallas_call | solution.py:25
  (39 shorter events, 0.2 us)
Async XLA Ops:
  0.6 10.6 %collective-permute-start = (bf16[12,4096]{1,0:T(8,128)(2,1)}, bf16[12,4096]{1,0:T(8,128)(2,1)S(1)}, u32[]{:S(2)}, u32[]{:S(2)}) collective-permute-start(bf16[12,4096]{1,0:T(8,128)(2,1)} %refs_3_.1), channel_id=1, source_target_pairs={{0,16},{1,17},{2,18},{3,19},{4,20},{5,21},{6,22},{7,23},{8,10},{9,... | collective-permute-start | bytes 294920 | tf_op jit(solution)/shard_map/ppermute | solution.py:48
  3.7 7.5 %collective-permute-start.2 = (bf16[12,4096]{1,0:T(8,128)(2,1)}, bf16[12,4096]{1,0:T(8,128)(2,1)S(1)}, u32[]{:S(2)}, u32[]{:S(2)}) collective-permute-start(bf16[12,4096]{1,0:T(8,128)(2,1)} %refs_3_.1), channel_id=1, source_target_pairs={{0,16},{1,17},{2,18},{3,19},{4,20},{5,21},{6,22},{7,23},{8,14},{9,... | collective-permute-start | bytes 294920 | tf_op jit(solution)/shard_map/ppermute | solution.py:48
  3.8 7.5 %collective-permute-start.1 = (bf16[12,4096]{1,0:T(8,128)(2,1)}, bf16[12,4096]{1,0:T(8,128)(2,1)S(1)}, u32[]{:S(2)}, u32[]{:S(2)}) collective-permute-start(bf16[12,4096]{1,0:T(8,128)(2,1)} %refs_3_.1), channel_id=1, source_target_pairs={{0,16},{1,17},{2,18},{3,19},{4,20},{5,21},{6,22},{7,23},{8,12},{9,... | collective-permute-start | bytes 294920 | tf_op jit(solution)/shard_map/ppermute | solution.py:48
  5.7 1.0 %copy-start.4 = (bf16[1,128,2048]{2,1,0:T(8,128)(2,1)S(1)}, bf16[1,128,2048]{2,1,0:T(8,128)(2,1)}, u32[]{:S(2)}) copy-start(bf16[1,128,2048]{2,1,0:T(8,128)(2,1)} %param.16) | copy-start | bytes 1572868
  6.8 0.9 %copy-start.5 = (bf16[12,4096]{1,0:T(8,128)(2,1)S(1)}, bf16[12,4096]{1,0:T(8,128)(2,1)}, u32[]{:S(2)}) copy-start(bf16[12,4096]{1,0:T(8,128)(2,1)} %refs_3_.1) | copy-start | bytes 294916
  7.7 0.8 %copy-start.6 = (bf16[1,16,2048]{2,1,0:T(8,128)(2,1)S(1)}, bf16[1,16,2048]{2,1,0:T(8,128)(2,1)}, u32[]{:S(2)}) copy-start(bf16[1,16,2048]{2,1,0:T(8,128)(2,1)} %param.19) | copy-start | bytes 196612
  8.5 0.8 %copy-start.7 = (bf16[4,4096]{1,0:T(4,128)(2,1)S(1)}, bf16[4,4096]{1,0:T(4,128)(2,1)}, u32[]{:S(2)}) copy-start(bf16[4,4096]{1,0:T(4,128)(2,1)} %refs_2_.1) | copy-start | bytes 98308
  9.3 0.7 copy-start.8
  9.9 0.7 copy-start.9
  10.6 5.8 %copy-start = (bf16[1,4096,2048]{2,1,0:T(8,128)(2,1)S(1)}, bf16[1,4096,2048]{2,1,0:T(8,128)(2,1)}, u32[]{:S(2)}) copy-start(bf16[1,4096,2048]{2,1,0:T(8,128)(2,1)} %param.17) | copy-start | bytes 50331652
  16.6 1.6 %copy-start.1 = (bf16[1,2048,16]{1,2,0:T(8,128)(2,1)S(1)}, bf16[1,2048,16]{1,2,0:T(8,128)(2,1)}, u32[]{:S(2)}) copy-start(bf16[1,2048,16]{1,2,0:T(8,128)(2,1)} %param.18) | copy-start | bytes 196612
  16.6 1.6 %collective-permute-start.3 = (bf16[144,1024]{1,0:T(8,128)(2,1)S(1)}, bf16[144,1024]{1,0:T(8,128)(2,1)S(1)}, u32[]{:S(2)}, u32[]{:S(2)}) collective-permute-start(bf16[144,1024]{1,0:T(8,128)(2,1)S(1)} %get-tuple-element.43.after_ref), channel_id=1, source_target_pairs={{0,8},{1,9},{2,10},{3,11},{4,12},{5,13},{6,14},{7,15},{8,0},{9,1},... | collective-permute-start | bytes 884744 | tf_op jit(solution)/shard_map/ppermute | solution.py:48
  16.6 1.9 %collective-permute-start.5 = (bf16[128,1024]{1,0:T(8,128)(2,1)S(1)}, bf16[128,1024]{1,0:T(8,128)(2,1)S(1)}, u32[]{:S(2)}, u32[]{:S(2)}) collective-permute-start(bf16[128,1024]{1,0:T(8,128)(2,1)S(1)} %shard_map.119), channel_id=1, source_target_pairs={{0,8},{1,9},{2,10},{3,11},{4,12},{5,13},{6,14},{7,15},{8,0},{9,1},... | collective-permute-start | bytes 786440 | tf_op jit(solution)/shard_map/ppermute | solution.py:48
  18.2 1.5 %collective-permute-start.4 = (bf16[128,1024]{1,0:T(8,128)(2,1)S(1)}, bf16[128,1024]{1,0:T(8,128)(2,1)S(1)}, u32[]{:S(2)}, u32[]{:S(2)}) collective-permute-start(bf16[128,1024]{1,0:T(8,128)(2,1)S(1)} %shard_map.116.refs_6_), channel_id=1, source_target_pairs={{0,8},{1,9},{2,10},{3,11},{4,12},{5,13},{6,14},{7,15},{8,0},{9,1},... | collective-permute-start | bytes 786440 | tf_op jit(solution)/shard_map/ppermute | solution.py:48
  18.6 1.5 %collective-permute-start.6 = (bf16[128,1024]{1,0:T(8,128)(2,1)S(1)}, bf16[128,1024]{1,0:T(8,128)(2,1)S(1)}, u32[]{:S(2)}, u32[]{:S(2)}) collective-permute-start(bf16[128,1024]{1,0:T(8,128)(2,1)S(1)} %shard_map.120.refs_6_), channel_id=1, source_target_pairs={{0,8},{1,9},{2,10},{3,11},{4,12},{5,13},{6,14},{7,15},{8,0},{9,1},... | collective-permute-start | bytes 786440 | tf_op jit(solution)/shard_map/ppermute | solution.py:48
  20.1 1.6 %collective-permute-start.7 = (bf16[144,1024]{1,0:T(8,128)(2,1)S(1)}, bf16[144,1024]{1,0:T(8,128)(2,1)S(1)}, u32[]{:S(2)}, u32[]{:S(2)}) collective-permute-start(bf16[144,1024]{1,0:T(8,128)(2,1)S(1)} %get-tuple-element.49.after_ref), channel_id=1, source_target_pairs={{0,8},{1,9},{2,10},{3,11},{4,12},{5,13},{6,14},{7,15},{8,0},{9,1},... | collective-permute-start | bytes 884744 | tf_op jit(solution)/shard_map/ppermute | solution.py:48
  20.3 3.1 %collective-permute-start.9 = (bf16[128,1024]{1,0:T(8,128)(2,1)S(1)}, bf16[128,1024]{1,0:T(8,128)(2,1)S(1)}, u32[]{:S(2)}, u32[]{:S(2)}) collective-permute-start(bf16[128,1024]{1,0:T(8,128)(2,1)S(1)} %shard_map.126), channel_id=1, source_target_pairs={{0,8},{1,9},{2,10},{3,11},{4,12},{5,13},{6,14},{7,15},{8,0},{9,1},... | collective-permute-start | bytes 786440 | tf_op jit(solution)/shard_map/ppermute | solution.py:48
  21.8 6.4 %collective-permute-start.8 = (bf16[128,1024]{1,0:T(8,128)(2,1)S(1)}, bf16[128,1024]{1,0:T(8,128)(2,1)S(1)}, u32[]{:S(2)}, u32[]{:S(2)}) collective-permute-start(bf16[128,1024]{1,0:T(8,128)(2,1)S(1)} %shard_map.123.refs_6_), channel_id=1, source_target_pairs={{0,2},{1,3},{2,0},{3,1},{4,6},{5,7},{6,4},{7,5},{8,16},{9,17},{10,... | collective-permute-start | bytes 786440 | tf_op jit(solution)/shard_map/ppermute | solution.py:48
  23.5 7.6 %collective-permute-start.10 = (bf16[128,1024]{1,0:T(8,128)(2,1)S(1)}, bf16[128,1024]{1,0:T(8,128)(2,1)S(1)}, u32[]{:S(2)}, u32[]{:S(2)}) collective-permute-start(bf16[128,1024]{1,0:T(8,128)(2,1)S(1)} %shard_map.127.refs_6_), channel_id=1, source_target_pairs={{0,2},{1,3},{2,0},{3,1},{4,6},{5,7},{6,4},{7,5},{8,16},{9,17},{10,... | collective-permute-start | bytes 786440 | tf_op jit(solution)/shard_map/ppermute | solution.py:48
  31.1 6.8 %collective-permute-start.11 = (bf16[144,1024]{1,0:T(8,128)(2,1)S(1)}, bf16[144,1024]{1,0:T(8,128)(2,1)S(1)}, u32[]{:S(2)}, u32[]{:S(2)}) collective-permute-start(bf16[144,1024]{1,0:T(8,128)(2,1)S(1)} %get-tuple-element.54.after_ref), channel_id=1, source_target_pairs={{0,2},{1,3},{2,0},{3,1},{4,6},{5,7},{6,4},{7,5},{8,9},{9,8},{10,11... | collective-permute-start | bytes 884744 | tf_op jit(solution)/shard_map/ppermute | solution.py:48
  32.7 19.2 %collective-permute-start.13 = (bf16[128,1024]{1,0:T(8,128)(2,1)S(1)}, bf16[128,1024]{1,0:T(8,128)(2,1)S(1)}, u32[]{:S(2)}, u32[]{:S(2)}) collective-permute-start(bf16[128,1024]{1,0:T(8,128)(2,1)S(1)} %shard_map.132), channel_id=1, source_target_pairs={{0,2},{1,3},{2,0},{3,1},{4,6},{5,7},{6,4},{7,5},{8,9},{9,8},{10,11... | collective-permute-start | bytes 786440 | tf_op jit(solution)/shard_map/ppermute | solution.py:48
  37.9 16.8 %collective-permute-start.12 = (bf16[128,1024]{1,0:T(8,128)(2,1)S(1)}, bf16[128,1024]{1,0:T(8,128)(2,1)S(1)}, u32[]{:S(2)}, u32[]{:S(2)}) collective-permute-start(bf16[128,1024]{1,0:T(8,128)(2,1)S(1)} %shard_map.130.refs_7_), channel_id=1, source_target_pairs={{0,8},{1,9},{2,10},{3,11},{4,12},{5,13},{6,14},{7,15},{8,0},{9,1},... | collective-permute-start | bytes 786440 | tf_op jit(solution)/shard_map/ppermute | solution.py:48
  51.9 9.7 %copy-start.2 = (bf16[1,128,2048]{2,1,0:T(8,128)(2,1)S(1)}, bf16[1,128,2048]{2,1,0:T(8,128)(2,1)}, u32[]{:S(2)}) copy-start(bf16[1,128,2048]{2,1,0:T(8,128)(2,1)} %param.14) | copy-start | bytes 1572868
  51.9 9.7 %copy-start.3 = (bf16[1,128,16]{1,2,0:T(8,128)(2,1)S(1)}, bf16[1,128,16]{1,2,0:T(8,128)(2,1)}, u32[]{:S(2)}) copy-start(bf16[1,128,16]{1,2,0:T(8,128)(2,1)} %param.15) | copy-start | bytes 12292
  51.9 4.3 %collective-permute-start.14 = (bf16[128,1024]{1,0:T(8,128)(2,1)S(1)}, bf16[128,1024]{1,0:T(8,128)(2,1)S(1)}, u32[]{:S(2)}, u32[]{:S(2)}) collective-permute-start(bf16[128,1024]{1,0:T(8,128)(2,1)S(1)} %shard_map.133.refs_8_), channel_id=1, source_target_pairs={{0,8},{1,9},{2,10},{3,11},{4,12},{5,13},{6,14},{7,15},{8,0},{9,1},... | collective-permute-start | bytes 786440 | tf_op jit(solution)/shard_map/ppermute | solution.py:48
  57.9 3.7 %collective-permute-start.15 = (bf16[16,128]{1,0:T(8,128)(2,1)S(1)}, bf16[16,128]{1,0:T(8,128)(2,1)S(1)}, u32[]{:S(2)}, u32[]{:S(2)}) collective-permute-start(bf16[16,128]{1,0:T(8,128)(2,1)S(1)} %get-tuple-element.58.refs_4_), channel_id=1, source_target_pairs={{0,1},{1,0},{2,3},{3,2},{4,5},{5,4},{6,7},{7,6},{8,9},{9,8},{10,11... | collective-permute-start | bytes 12296 | tf_op jit(solution)/shard_map/ppermute | solution.py:48
  61.8 5.3 %collective-permute-start.17 = (bf16[16,2048]{1,0:T(8,128)(2,1)S(1)}, bf16[16,2048]{1,0:T(8,128)(2,1)S(1)}, u32[]{:S(2)}, u32[]{:S(2)}) collective-permute-start(bf16[16,2048]{1,0:T(8,128)(2,1)S(1)} %get-tuple-element.61), channel_id=1, source_target_pairs={{0,4},{1,5},{2,6},{3,7},{4,0},{5,1},{6,2},{7,3},{8,12},{9,13},{10,... | collective-permute-start | bytes 196616 | tf_op jit(solution)/shard_map/ppermute | solution.py:48
  64.4 9.2 %collective-permute-start.16 = (bf16[128,2048]{1,0:T(8,128)(2,1)S(1)}, bf16[128,2048]{1,0:T(8,128)(2,1)S(1)}, u32[]{:S(2)}, u32[]{:S(2)}) collective-permute-start(bf16[128,2048]{1,0:T(8,128)(2,1)S(1)} %get-tuple-element.59), channel_id=1, source_target_pairs={{0,1},{1,0},{2,3},{3,2},{4,5},{5,4},{6,7},{7,6},{8,10},{9,11},{10,... | collective-permute-start | bytes 1572872 | tf_op jit(solution)/shard_map/ppermute | solution.py:48
  67.2 5.1 %collective-permute-start.18 = (bf16[8,2048]{1,0:T(8,128)(2,1)S(1)}, bf16[8,2048]{1,0:T(8,128)(2,1)S(1)}, u32[]{:S(2)}, u32[]{:S(2)}) collective-permute-start(bf16[8,2048]{1,0:T(8,128)(2,1)S(1)} %get-tuple-element.63), channel_id=1, source_target_pairs={{0,2},{1,3},{2,0},{3,1},{4,6},{5,7},{6,4},{7,5},{8,10},{9,11},{10,... | collective-permute-start | bytes 98312 | tf_op jit(solution)/shard_map/ppermute | solution.py:48

commit v3 on v2

--- a/solution.py
+++ b/solution.py
@@ -72,13 +72,14 @@
     return partner
 
 
-def gather_pairing(step):
-    def partner(s, d, t):
-        if s % 2:
-            return (s, d ^ step, t)
-        return (s ^ 2, d, t)
-
-    return partner
+def gather_pieces(piece, sizes):
+    def fetch(s, d, t):
+        return (s, d ^ (1, 3, 2, 1)[s], t)
+
+    fetched = exchange(piece, fetch, sizes)
+    beside = exchange(fetched, lambda s, d, t: (s ^ 1, d, t), sizes)
+    across = exchange(fetched, lambda s, d, t: (s ^ 2, d, t), sizes)
+    return [piece, fetched, beside, across]
 
 
 def branch(g_ref, slope_ref, chunk):
@@ -129,19 +130,7 @@
         out_ref[: total.shape[0], at : at + tile] = total.astype(out_ref.dtype)
 
 
-def setup_kernel(count, *refs):
-    sources = refs[:count]
-    scale_ref, at_ref = refs[count : count + 2]
-    targets = refs[count + 2 : 2 * count]
-    positives_ref, counts_ref, semaphores = refs[2 * count :]
-    copies = [
-        pltpu.make_async_copy(source, target, semaphores.at[i])
-        for i, (source, target) in enumerate(zip(sources, (positives_ref, counts_ref, *targets)))
-    ]
-    for copy in copies:
-        copy.start()
-    copies[0].wait()
-    copies[1].wait()
+def setup_kernel(positives_ref, counts_ref, scale_ref, at_ref):
     queries = counts_ref.shape[0]
     length = scale_ref.shape[0] // queries
     position = lax.broadcasted_iota(jnp.int32, (length, scale_ref.shape[1]), 0)
@@ -154,33 +143,6 @@
         ) / live.astype(jnp.float32)
         positive = jnp.where(row == i, positives_ref[i], positive)
     at_ref[...] = positive
-    for copy in copies[2:]:
-        copy.wait()
-
-
-def setup(arrays, rows):
-    positives, counts, *held = arrays
-    outs = [
-        jax.ShapeDtypeStruct((rows, 128), jnp.float32),
-        jax.ShapeDtypeStruct((counts.shape[0], 128), jnp.int32),
-        *(jax.ShapeDtypeStruct(v.shape, v.dtype) for v in held),
-    ]
-    return pl.pallas_call(
-        functools.partial(setup_kernel, len(arrays)),
-        out_shape=outs,
-        in_specs=[pl.BlockSpec(memory_space=pltpu.HBM) for _ in arrays],
-        out_specs=[pl.BlockSpec(memory_space=pltpu.VMEM) for _ in outs],
-        scratch_shapes=[
-            pltpu.SMEM(positives.shape, positives.dtype),
-            pltpu.SMEM(counts.shape, counts.dtype),
-            pltpu.SemaphoreType.DMA((len(arrays),)),
-        ],
-        name="setup",
-        compiler_params=pltpu.CompilerParams(vmem_limit_bytes=VMEM_GRANT),
-        cost_estimate=pl.CostEstimate(
-            flops=COVER_FLOPS, bytes_accessed=1 << 20, transcendentals=0
-        ),
-    )(*arrays)
 
 
 def top_kernel(piece_count, bases, scale_ref, at_ref, query_ref, *refs):
@@ -277,6 +239,18 @@
     when_section(active, run, keep)
 
 
+def branch_kernel(active, g_ref, slope_ref, up_ref, h_in, inner_in, first_h, h_ref, inner_ref):
+    def run():
+        h_ref[...] = branch(g_ref, slope_ref, 1)
+        inner_ref[...] = inner_terms([first_h, h_ref], up_ref)
+
+    def keep():
+        h_ref[...] = h_in[...]
+        inner_ref[...] = inner_in[...]
+
+    when_section(active, run, keep)
+
+
 def later_cross_kernel(active, count, parts, offset, local, after_ref, weight_ref, *refs):
     del after_ref
     h_refs, rest = refs[: len(parts)], refs[len(parts) :]
@@ -391,23 +365,27 @@
     inner_shape = jax.ShapeDtypeStruct((rank, rows), jnp.bfloat16)
     matmul_flops = lambda depth, columns: 2 * rows * depth * columns
 
-    if few_replicas:
-        bases = list(range(replica_total))
-        pieces = [passage_embedded] + [
-            exchange(passage_embedded, gather_pairing(step), sizes)
-            for step in bases[1:]
-        ]
+    if (section_count, replica_total) == (4, 4):
+        bases = [0, 1, 2, 3]
+        pieces = gather_pieces(passage_embedded, sizes)
     else:
         bases = [None]
         pieces = [lax.all_gather(passage_embedded, "dp", axis=0, tiled=True)]
     pitch = -(-pieces[0].shape[0] // 16) * 16
-    scale, at, query_held, pieces[0], slope, up = setup(
-        (positives, counts, query_embedded, pieces[0], slope, up), rows
+    scale, at = vmem_call(
+        setup_kernel,
+        (
+            struct(128, jnp.float32),
+            jax.ShapeDtypeStruct((query_embedded.shape[0], 128), jnp.int32),
+        ),
+        (positives, counts),
+        COVER_FLOPS,
+        smem=(0, 1),
     )
     tops = vmem_call(
         functools.partial(top_kernel, len(pieces), bases),
         (struct(span),) * (2 * CHUNKS),
-        (scale, at, query_held, *pieces, slope),
+        (scale, at, query_embedded, *pieces, slope),
         0,
         scratch=[pltpu.VMEM((len(pieces) * pitch, passage_embedded.shape[1]), jnp.bfloat16)],
     )
@@ -439,12 +417,26 @@
                 (g[0], slope, h[0], weight),
                 matmul_flops(span, local) * len(others),
             )
-            second_h, inner, *crosses = vmem_call(
-                functools.partial(next_cross_kernel, active, 1 + len(others)),
-                (struct(span), inner_shape) + (payload,) * len(others),
-                (g[1], slope, up, h[1], inner, weight, first_h, *bases_held),
-                matmul_flops(span, width) * len(others),
-            )
+            if last:
+                second_h, inner = vmem_call(
+                    functools.partial(branch_kernel, active),
+                    (struct(span), inner_shape),
+                    (g[1], slope, up, h[1], inner, first_h),
+                    matmul_flops(span, rank),
+                )
+                crosses = vmem_call(
+                    functools.partial(later_cross_kernel, active, len(others), [1], 0, local),
+                    (struct(width),) * len(others),
+                    (inner, weight, second_h, *bases_held),
+                    matmul_flops(span, width) * len(others),
+                )
+            else:
+                second_h, inner, *crosses = vmem_call(
+                    functools.partial(next_cross_kernel, active, 1 + len(others)),
+                    (struct(span), inner_shape) + (payload,) * len(others),
+                    (g[1], slope, up, h[1], inner, weight, first_h, *bases_held),
+                    matmul_flops(span, width) * len(others),
+                )
             h = [first_h, second_h]
             parts, cross_h = [1], [second_h]
         received[0] = swap(crosses)
@@ -474,59 +466,44 @@
             )
             g_parts = g if last else [g[k]]
             kept = [] if results is None else results if last else [results[k]]
-            (total,) = vmem_call(
-                functools.partial(
-                    combine_kernel, active, offset, tensor_count, len(g_parts)
-                ),
-                (struct(width),),
-                (
-                    *g_parts,
-                    own,
-                    down,
-                    inner,
-                    *inner_others,
-                    *received[offset],
-                    *kept,
-                ),
-                matmul_flops(rank, width),
-            )
+            combine = functools.partial(
+                combine_kernel, active, offset, tensor_count, len(g_parts)
+            )
+            terms = (*g_parts, own, down, inner, *inner_others, *received[offset], *kept)
+            (total,) = vmem_call(combine, (struct(width),), terms, matmul_flops(rank, width))
             sums.append(total)
             if not last:
                 next_g.append(exchange(total, hop_pairing(active), sizes))
         results, g = sums, next_g
-    result = results[0]
 
     factor = ADAPTER_SCALE / (query_embedded.shape[0] * replica_total)
     halves = lambda n: (
         jax.ShapeDtypeStruct((n, local), jnp.float32),
         jax.ShapeDtypeStruct((n, local), jnp.bfloat16),
     )
-    sums = vmem_call(
+    parts = vmem_call(
         functools.partial(adapter_kernel, factor, tensor_count, CHUNKS, replica_total),
         halves(rank) if few_replicas else halves(2 * rank)[1:],
         (stored, saved, *h, inner, *inner_others),
         4 * rows * local * rank,
     )
     if few_replicas:
-        kept, sent = sums
+        kept, sent = parts
         step = replica_total // 2
         while True:
-            received = exchange(sent, lambda s, d, t, j=step: (s, d ^ j, t), sizes)
+            arrived = exchange(sent, lambda s, d, t, j=step: (s, d ^ j, t), sizes)
             if step == 1:
                 break
             step //= 2
             kept, sent = vmem_call(
-                functools.partial(fold_kernel, step),
-                halves(kept.shape[0] // 2),
-                (kept, received),
-                0,
-            )
-        reduced = kept + received.astype(jnp.float32)
+                functools.partial(fold_kernel, step), halves(kept.shape[0] // 2), (kept, arrived), 0
+            )
+        reduced = kept + arrived.astype(jnp.float32)
     else:
-        reduced = lax.psum_scatter(sums[0], "dp", scatter_dimension=0, tiled=True).astype(
+        reduced = lax.psum_scatter(parts[0], "dp", scatter_dimension=0, tiled=True).astype(
             jnp.float32
         )
-    return (result[None], reduced[None])
+    return (results[0][None], reduced[None])
 
 
 def solution(mesh):

time: 75.2 us -> 73 us (0.971)
  local copies, waits for them, and re-layouts: 9.3 us -> 1.35 us
  waiting for transfers between devices: 19.6 us -> 25.7 us
    unnamed x20, local copies, waits for them, and re-layouts: 9.3 us -> 1.35 us
    ppermute x19, waiting for transfers between devices: 19.6 us -> 25.7 us  [exchange(): return lax.ppermute(value, AXES, pairs)]
    pallas_call x27 -> x29, Pallas kernels: 8.58 us -> 9.23 us  [vmem_call(): pl.pallas_call(kernel, out_shape=outs, in_specs=[pl.BlockSpec(memory_spac...]
  transfers between devices with their start and end apart: 19 -> 19, of which waited for: 11 -> 12; matrix products, arithmetic and copies ran while one was open for 1% -> 1% of each run, Pallas kernels for 7% -> 9%
where the time goes in v3:
time: 73 us; the launch traced here: 72.8 us
  starting transfers between devices  35.1 us (48%)
  waiting for transfers between devices  25.7 us (35%)
  Pallas kernels  9.23 us (13%)
  local copies, waits for them, and re-layouts  1.35 us (2%)
  between operations  0.87 us (1%)
    ppermute x19, starting transfers between devices, exchange(): return lax.ppermute(value, AXES, pairs)  35.1 us
    ppermute x19, waiting for transfers between devices, exchange(): return lax.ppermute(value, AXES, pairs)  25.7 us
    pallas_call x29, Pallas kernels, vmem_call(): pl.pallas_call(kernel, out_shape=outs, in_specs=[pl.BlockSpec(memory_spac...  9.23 us
  transfers between devices with their start and end apart: 19, of which 12 were waited for; matrix products, arithmetic and copies ran while one was open for 1% of the time, Pallas kernels for 9%

profile of v3, /device:TPU:0, one launch (start us, length us, event | category | flops | bytes accessed | tf_op | source)
XLA Modules:
  0.0 72.8 jit_solution(10075376905386323659)
XLA Ops:
  0.7 3.1 %collective-permute-start = (bf16[12,4096]{1,0:T(8,128)(2,1)}, bf16[12,4096]{1,0:T(8,128)(2,1)S(1)}, u32[]{:S(2)}, u32[]{:S(2)}) collective-permute-start(bf16[12,4096]{1,0:T(8,128)(2,1)} %refs_0_.1), channel_id=1, source_target_pairs={{0,2},{1,3},{2,0},{3,1},{4,6},{5,7},{6,4},{7,5},{8,14},{9,15},{10,... | collective-permute-start | bytes 294920 | tf_op jit(solution)/shard_map/ppermute | solution.py:48
  3.8 4.6 %collective-permute-done.refs_1_ = bf16[12,4096]{1,0:T(8,128)(2,1)S(1)} collective-permute-done((bf16[12,4096]{1,0:T(8,128)(2,1)}, bf16[12,4096]{1,0:T(8,128)(2,1)S(1)}, u32[]{:S(2)}, u32[]{:S(2)}) %collective-permute-start) | collective-permute-done | bytes 98336 | tf_op jit(solution)/shard_map/ppermute | solution.py:48
  8.4 1.8 %collective-permute-start.2 = (bf16[12,4096]{1,0:T(8,128)(2,1)S(1)}, bf16[12,4096]{1,0:T(8,128)(2,1)S(1)}, u32[]{:S(2)}, u32[]{:S(2)}) collective-permute-start(bf16[12,4096]{1,0:T(8,128)(2,1)S(1)} %collective-permute-done.refs_1_), channel_id=1, source_target_pairs={{0,16},{1,17},{2,18},{3,19},{4,20},{5,21},{6,22},{7,23},{8,24},{9,... | collective-permute-start | bytes 294920 | tf_op jit(solution)/shard_map/ppermute | solution.py:48
  10.2 0.0 collective-permute-start.1
  10.2 0.7 copy-done.8
  10.9 0.7 copy-done.9
  11.5 0.6 shard_map.113
  12.1 1.5 %collective-permute-done.2.refs_3_ = bf16[12,4096]{1,0:T(8,128)(2,1)S(1)} collective-permute-done((bf16[12,4096]{1,0:T(8,128)(2,1)S(1)}, bf16[12,4096]{1,0:T(8,128)(2,1)S(1)}, u32[]{:S(2)}, u32[]{:S(2)}) %collective-permute-start.2) | collective-permute-done | bytes 98336 | tf_op jit(solution)/shard_map/ppermute | solution.py:48
  13.6 0.7 shard_map.114
  14.3 0.2 shard_map.116
  14.5 0.0 collective-permute-start.3
  14.5 0.5 collective-permute-start.5
  15.0 1.1 %collective-permute-done.3.refs_4_.refs_5_ = bf16[144,1024]{1,0:T(8,128)(2,1)S(1)} collective-permute-done((bf16[144,1024]{1,0:T(8,128)(2,1)S(1)}, bf16[144,1024]{1,0:T(8,128)(2,1)S(1)}, u32[]{:S(2)}, u32[]{:S(2)}) %collective-permute-start.3) | collective-permute-done | bytes 294944 | tf_op jit(solution)/shard_map/ppermute | solution.py:48
  16.1 0.1 collective-permute-start.4
  16.2 0.2 collective-permute-done.5.refs_5_
  16.5 0.1 collective-permute-start.6
  16.6 1.0 %collective-permute-done.4.g_ref.refs_0_ = bf16[128,1024]{1,0:T(8,128)(2,1)S(1)} collective-permute-done((bf16[128,1024]{1,0:T(8,128)(2,1)S(1)}, bf16[128,1024]{1,0:T(8,128)(2,1)S(1)}, u32[]{:S(2)}, u32[]{:S(2)}) %collective-permute-start.4) | collective-permute-done | bytes 262176 | tf_op jit(solution)/shard_map/ppermute | solution.py:48
  17.7 0.4 collective-permute-done.6.g_ref.refs_0_
  18.0 0.2 collective-permute-start.7
  18.2 0.4 collective-permute-start.9
  18.6 1.1 %collective-permute-done.7.refs_4_.refs_5_ = bf16[144,1024]{1,0:T(8,128)(2,1)S(1)} collective-permute-done((bf16[144,1024]{1,0:T(8,128)(2,1)S(1)}, bf16[144,1024]{1,0:T(8,128)(2,1)S(1)}, u32[]{:S(2)}, u32[]{:S(2)}) %collective-permute-start.7) | collective-permute-done | bytes 294944 | tf_op jit(solution)/shard_map/ppermute | solution.py:48
  19.7 1.5 %collective-permute-start.8 = (bf16[128,1024]{1,0:T(8,128)(2,1)S(1)}, bf16[128,1024]{1,0:T(8,128)(2,1)S(1)}, u32[]{:S(2)}, u32[]{:S(2)}) collective-permute-start(bf16[128,1024]{1,0:T(8,128)(2,1)S(1)} %shard_map.124.refs_6_), channel_id=1, source_target_pairs={{0,2},{1,3},{2,0},{3,1},{4,6},{5,7},{6,4},{7,5},{8,16},{9,17},{10,... | collective-permute-start | bytes 786440 | tf_op jit(solution)/shard_map/ppermute | solution.py:48
  21.2 0.7 collective-permute-start.10
  21.9 4.3 %collective-permute-done.8.g_ref.refs_0_ = bf16[128,1024]{1,0:T(8,128)(2,1)S(1)} collective-permute-done((bf16[128,1024]{1,0:T(8,128)(2,1)S(1)}, bf16[128,1024]{1,0:T(8,128)(2,1)S(1)}, u32[]{:S(2)}, u32[]{:S(2)}) %collective-permute-start.8) | collective-permute-done | bytes 262176 | tf_op jit(solution)/shard_map/ppermute | solution.py:48
  26.2 2.8 %collective-permute-done.10.g_ref.refs_0_ = bf16[128,1024]{1,0:T(8,128)(2,1)S(1)} collective-permute-done((bf16[128,1024]{1,0:T(8,128)(2,1)S(1)}, bf16[128,1024]{1,0:T(8,128)(2,1)S(1)}, u32[]{:S(2)}, u32[]{:S(2)}) %collective-permute-start.10) | collective-permute-done | bytes 262176 | tf_op jit(solution)/shard_map/ppermute | solution.py:48
  29.0 1.5 %collective-permute-start.11 = (bf16[144,1024]{1,0:T(8,128)(2,1)S(1)}, bf16[144,1024]{1,0:T(8,128)(2,1)S(1)}, u32[]{:S(2)}, u32[]{:S(2)}) collective-permute-start(bf16[144,1024]{1,0:T(8,128)(2,1)S(1)} %get-tuple-element.45.after_ref), channel_id=1, source_target_pairs={{0,2},{1,3},{2,0},{3,1},{4,6},{5,7},{6,4},{7,5},{8,9},{9,8},{10,11... | collective-permute-start | bytes 884744 | tf_op jit(solution)/shard_map/ppermute | solution.py:48
  30.4 0.6 collective-permute-start.13
  31.1 4.7 %collective-permute-done.11.refs_4_.refs_5_ = bf16[144,1024]{1,0:T(8,128)(2,1)S(1)} collective-permute-done((bf16[144,1024]{1,0:T(8,128)(2,1)S(1)}, bf16[144,1024]{1,0:T(8,128)(2,1)S(1)}, u32[]{:S(2)}, u32[]{:S(2)}) %collective-permute-start.11) | collective-permute-done | bytes 294944 | tf_op jit(solution)/shard_map/ppermute | solution.py:48
  35.8 0.0 copy-start.4
  35.8 0.0 copy-start.7
  35.8 13.5 %collective-permute-start.12 = (bf16[128,1024]{1,0:T(8,128)(2,1)S(1)}, bf16[128,1024]{1,0:T(8,128)(2,1)S(1)}, u32[]{:S(2)}, u32[]{:S(2)}) collective-permute-start(bf16[128,1024]{1,0:T(8,128)(2,1)S(1)} %shard_map.131.refs_7_), channel_id=1, source_target_pairs={{0,8},{1,9},{2,10},{3,11},{4,12},{5,13},{6,14},{7,15},{8,0},{9,1},... | collective-permute-start | bytes 786440 | tf_op jit(solution)/shard_map/ppermute | solution.py:48
  49.3 0.0 collective-permute-done.13.refs_5_
  49.3 2.8 %collective-permute-start.14 = (bf16[128,1024]{1,0:T(8,128)(2,1)S(1)}, bf16[128,1024]{1,0:T(8,128)(2,1)S(1)}, u32[]{:S(2)}, u32[]{:S(2)}) collective-permute-start(bf16[128,1024]{1,0:T(8,128)(2,1)S(1)} %shard_map.134.refs_8_), channel_id=1, source_target_pairs={{0,8},{1,9},{2,10},{3,11},{4,12},{5,13},{6,14},{7,15},{8,0},{9,1},... | collective-permute-start | bytes 786440 | tf_op jit(solution)/shard_map/ppermute | solution.py:48
  52.1 1.5 %shard_map.135 = (bf16[128,1024]{1,0:T(8,128)(2,1)S(1)}, f32[128,2048]{1,0:T(8,128)S(1)}) custom-call(bf16[128,1024]{1,0:T(8,128)(2,1)S(1)} %collective-permute-done.12.g_ref.refs_0_, bf16[128,2048]{1,0:T(8,128)(2,1)S(1)} %bitcast.35, bf16[128,1024]{1,0:T(8,128)(2,1)S(1)} %get-tuple-element.41.refs_0_.h_in, bf16[4096,2048]{1,0:T(8,128)(2,1)S(1)} %bitcast.27), custom_call_target="tpu_custom_call" | custom-call | flops 536870912 | bytes 19136512 | tf_op jit(solution)/shard_map/pallas_call | solution.py:25
  53.6 0.2 shard_map.136
  53.8 1.5 %collective-permute-start.15 = (bf16[16,128]{1,0:T(8,128)(2,1)S(1)}, bf16[16,128]{1,0:T(8,128)(2,1)S(1)}, u32[]{:S(2)}, u32[]{:S(2)}) collective-permute-start(bf16[16,128]{1,0:T(8,128)(2,1)S(1)} %get-tuple-element.48.after_ref.refs_4_), channel_id=1, source_target_pairs={{0,1},{1,0},{2,3},{3,2},{4,5},{5,4},{6,7},{7,6},{8,9},{9,8},{10,11... | collective-permute-start | bytes 12296 | tf_op jit(solution)/shard_map/ppermute | solution.py:48
  55.4 2.1 %collective-permute-done.15.refs_5_ = bf16[16,128]{1,0:T(8,128)(2,1)S(1)} collective-permute-done((bf16[16,128]{1,0:T(8,128)(2,1)S(1)}, bf16[16,128]{1,0:T(8,128)(2,1)S(1)}, u32[]{:S(2)}, u32[]{:S(2)}) %collective-permute-start.15) | collective-permute-done | bytes 4128 | tf_op jit(solution)/shard_map/ppermute | solution.py:48
  57.5 0.2 shard_map.140
  57.7 3.1 %collective-permute-start.17 = (bf16[16,2048]{1,0:T(8,128)(2,1)S(1)}, bf16[16,2048]{1,0:T(8,128)(2,1)S(1)}, u32[]{:S(2)}, u32[]{:S(2)}) collective-permute-start(bf16[16,2048]{1,0:T(8,128)(2,1)S(1)} %get-tuple-element.51), channel_id=1, source_target_pairs={{0,4},{1,5},{2,6},{3,7},{4,0},{5,1},{6,2},{7,3},{8,12},{9,13},{10,... | collective-permute-start | bytes 196616 | tf_op jit(solution)/shard_map/ppermute | solution.py:48
  60.9 1.5 %shard_map.138 = bf16[128,2048]{1,0:T(8,128)(2,1)S(1)} custom-call(bf16[16,128]{1,0:T(8,128)(2,1)S(1)} %get-tuple-element.48.after_ref.refs_4_, bf16[4096,2048]{1,0:T(8,128)(2,1)S(1)} %bitcast.28, bf16[128,1024]{1,0:T(8,128)(2,1)S(1)} %get-tuple-element.47.refs_1_.refs_0_.refs_3_, f32[128,2048]{1,0:T(8,128)S(1)} %get-tuple-element.49.refs_1_), custom_call_target="tpu_custom_call" | custom-call | flops 536870912 | bytes 18616320 | tf_op jit(solution)/shard_map/pallas_call | solution.py:25
  62.4 1.6 %collective-permute-start.16 = (bf16[128,2048]{1,0:T(8,128)(2,1)S(1)}, bf16[128,2048]{1,0:T(8,128)(2,1)S(1)}, u32[]{:S(2)}, u32[]{:S(2)}) collective-permute-start(bf16[128,2048]{1,0:T(8,128)(2,1)S(1)} %shard_map.138), channel_id=1, source_target_pairs={{0,1},{1,0},{2,3},{3,2},{4,5},{5,4},{6,7},{7,6},{8,10},{9,11},{10,... | collective-permute-start | bytes 1572872 | tf_op jit(solution)/shard_map/ppermute | solution.py:48
  63.9 0.0 collective-permute-done.17.received_ref
  64.0 2.1 %collective-permute-start.18 = (bf16[8,2048]{1,0:T(8,128)(2,1)S(1)}, bf16[8,2048]{1,0:T(8,128)(2,1)S(1)}, u32[]{:S(2)}, u32[]{:S(2)}) collective-permute-start(bf16[8,2048]{1,0:T(8,128)(2,1)S(1)} %get-tuple-element.53), channel_id=1, source_target_pairs={{0,2},{1,3},{2,0},{3,1},{4,6},{5,7},{6,4},{7,5},{8,10},{9,11},{10,... | collective-permute-start | bytes 98312 | tf_op jit(solution)/shard_map/ppermute | solution.py:48
  66.1 2.9 %shard_map.137.refs_2_ = bf16[128,2048]{1,0:T(8,128)(2,1)S(1)} custom-call(bf16[4096,2048]{1,0:T(8,128)(2,1)S(1)} %bitcast.29, bf16[128,1024]{1,0:T(8,128)(2,1)S(1)} %get-tuple-element.46.first_h.refs_0_.refs_2_, bf16[128,1024]{1,0:T(8,128)(2,1)S(1)} %get-tuple-element.47.refs_1_.refs_0_.refs_3_), custom_call_target="tpu_custom_call" | custom-call | flops 1073741824 | bytes 17825792 | tf_op jit(solution)/shard_map/pallas_call | solution.py:25
  68.9 0.0 collective-permute-done.18
  68.9 0.6 add_bitcast_fusion
  69.6 2.0 %collective-permute-done.16.refs_6_ = bf16[128,2048]{1,0:T(8,128)(2,1)S(1)} collective-permute-done((bf16[128,2048]{1,0:T(8,128)(2,1)S(1)}, bf16[128,2048]{1,0:T(8,128)(2,1)S(1)}, u32[]{:S(2)}, u32[]{:S(2)}) %collective-permute-start.16) | collective-permute-done | bytes 524320 | tf_op jit(solution)/shard_map/ppermute | solution.py:48
  71.6 1.2 %shard_map.139 = bf16[128,2048]{1,0:T(8,128)(2,1)} custom-call(bf16[128,1024]{1,0:T(8,128)(2,1)S(1)} %collective-permute-done.12.g_ref.refs_0_, bf16[128,1024]{1,0:T(8,128)(2,1)S(1)} %collective-permute-done.14.g_ref.refs_1_, bf16[128,2048]{1,0:T(8,128)(2,1)S(1)} %shard_map.137.refs_2_, bf16[16,2048]{1,0:T(8,128)(2,1)S(1)} %bitcast.43, ...), custom_call_target="tpu_custom_call" | custom-call | flops 8388608 | bytes 2695168 | tf_op jit(solution)/shard_map/pallas_call | solution.py:25
  (40 shorter events, 0.2 us)
Async XLA Ops:
  0.6 12.9 %copy-start.5 = (bf16[12,4096]{1,0:T(8,128)(2,1)S(1)}, bf16[12,4096]{1,0:T(8,128)(2,1)}, u32[]{:S(2)}) copy-start(bf16[12,4096]{1,0:T(8,128)(2,1)} %refs_0_.1) | copy-start | bytes 294916
  0.6 12.9 %copy-start.1 = (bf16[1,128,2048]{2,1,0:T(8,128)(2,1)S(1)}, bf16[1,128,2048]{2,1,0:T(8,128)(2,1)}, u32[]{:S(2)}) copy-start(bf16[1,128,2048]{2,1,0:T(8,128)(2,1)} %param.16) | copy-start | bytes 1572868
  0.7 12.9 %copy-start.6 = (bf16[4,4096]{1,0:T(4,128)(2,1)S(1)}, bf16[4,4096]{1,0:T(4,128)(2,1)}, u32[]{:S(2)}) copy-start(bf16[4,4096]{1,0:T(4,128)(2,1)} %query_ref.1) | copy-start | bytes 98308
  0.7 13.6 %copy-start.3 = (bf16[1,16,2048]{2,1,0:T(8,128)(2,1)S(1)}, bf16[1,16,2048]{2,1,0:T(8,128)(2,1)}, u32[]{:S(2)}) copy-start(bf16[1,16,2048]{2,1,0:T(8,128)(2,1)} %param.19) | copy-start | bytes 196612
  0.7 13.6 %copy-start = (bf16[1,4096,2048]{2,1,0:T(8,128)(2,1)S(1)}, bf16[1,4096,2048]{2,1,0:T(8,128)(2,1)}, u32[]{:S(2)}) copy-start(bf16[1,4096,2048]{2,1,0:T(8,128)(2,1)} %param.17) | copy-start | bytes 50331652
  0.7 7.7 %collective-permute-start = (bf16[12,4096]{1,0:T(8,128)(2,1)}, bf16[12,4096]{1,0:T(8,128)(2,1)S(1)}, u32[]{:S(2)}, u32[]{:S(2)}) collective-permute-start(bf16[12,4096]{1,0:T(8,128)(2,1)} %refs_0_.1), channel_id=1, source_target_pairs={{0,2},{1,3},{2,0},{3,1},{4,6},{5,7},{6,4},{7,5},{8,14},{9,15},{10,... | collective-permute-start | bytes 294920 | tf_op jit(solution)/shard_map/ppermute | solution.py:48
  8.4 5.2 %collective-permute-start.2 = (bf16[12,4096]{1,0:T(8,128)(2,1)S(1)}, bf16[12,4096]{1,0:T(8,128)(2,1)S(1)}, u32[]{:S(2)}, u32[]{:S(2)}) collective-permute-start(bf16[12,4096]{1,0:T(8,128)(2,1)S(1)} %collective-permute-done.refs_1_), channel_id=1, source_target_pairs={{0,16},{1,17},{2,18},{3,19},{4,20},{5,21},{6,22},{7,23},{8,24},{9,... | collective-permute-start | bytes 294920 | tf_op jit(solution)/shard_map/ppermute | solution.py:48
  10.2 3.3 %collective-permute-start.1 = (bf16[12,4096]{1,0:T(8,128)(2,1)S(1)}, bf16[12,4096]{1,0:T(8,128)(2,1)S(1)}, u32[]{:S(2)}, u32[]{:S(2)}) collective-permute-start(bf16[12,4096]{1,0:T(8,128)(2,1)S(1)} %collective-permute-done.refs_1_), channel_id=1, source_target_pairs={{0,8},{1,9},{2,10},{3,11},{4,12},{5,13},{6,14},{7,15},{8,0},{9,1},... | collective-permute-start | bytes 294920 | tf_op jit(solution)/shard_map/ppermute | solution.py:48
  10.2 0.7 copy-start.8
  10.9 0.7 copy-start.9
  14.5 1.6 %copy-start.2 = (bf16[1,2048,16]{1,2,0:T(8,128)(2,1)S(1)}, bf16[1,2048,16]{1,2,0:T(8,128)(2,1)}, u32[]{:S(2)}) copy-start(bf16[1,2048,16]{1,2,0:T(8,128)(2,1)} %param.18) | copy-start | bytes 196612
  14.5 1.6 %collective-permute-start.3 = (bf16[144,1024]{1,0:T(8,128)(2,1)S(1)}, bf16[144,1024]{1,0:T(8,128)(2,1)S(1)}, u32[]{:S(2)}, u32[]{:S(2)}) collective-permute-start(bf16[144,1024]{1,0:T(8,128)(2,1)S(1)} %get-tuple-element.34.after_ref), channel_id=1, source_target_pairs={{0,8},{1,9},{2,10},{3,11},{4,12},{5,13},{6,14},{7,15},{8,0},{9,1},... | collective-permute-start | bytes 884744 | tf_op jit(solution)/shard_map/ppermute | solution.py:48
  14.5 1.9 %collective-permute-start.5 = (bf16[128,1024]{1,0:T(8,128)(2,1)S(1)}, bf16[128,1024]{1,0:T(8,128)(2,1)S(1)}, u32[]{:S(2)}, u32[]{:S(2)}) collective-permute-start(bf16[128,1024]{1,0:T(8,128)(2,1)S(1)} %shard_map.120), channel_id=1, source_target_pairs={{0,8},{1,9},{2,10},{3,11},{4,12},{5,13},{6,14},{7,15},{8,0},{9,1},... | collective-permute-start | bytes 786440 | tf_op jit(solution)/shard_map/ppermute | solution.py:48
  16.1 1.5 %collective-permute-start.4 = (bf16[128,1024]{1,0:T(8,128)(2,1)S(1)}, bf16[128,1024]{1,0:T(8,128)(2,1)S(1)}, u32[]{:S(2)}, u32[]{:S(2)}) collective-permute-start(bf16[128,1024]{1,0:T(8,128)(2,1)S(1)} %shard_map.117.refs_6_), channel_id=1, source_target_pairs={{0,8},{1,9},{2,10},{3,11},{4,12},{5,13},{6,14},{7,15},{8,0},{9,1},... | collective-permute-start | bytes 786440 | tf_op jit(solution)/shard_map/ppermute | solution.py:48
  16.5 1.5 %collective-permute-start.6 = (bf16[128,1024]{1,0:T(8,128)(2,1)S(1)}, bf16[128,1024]{1,0:T(8,128)(2,1)S(1)}, u32[]{:S(2)}, u32[]{:S(2)}) collective-permute-start(bf16[128,1024]{1,0:T(8,128)(2,1)S(1)} %shard_map.121.refs_6_), channel_id=1, source_target_pairs={{0,8},{1,9},{2,10},{3,11},{4,12},{5,13},{6,14},{7,15},{8,0},{9,1},... | collective-permute-start | bytes 786440 | tf_op jit(solution)/shard_map/ppermute | solution.py:48
  18.0 1.6 %collective-permute-start.7 = (bf16[144,1024]{1,0:T(8,128)(2,1)S(1)}, bf16[144,1024]{1,0:T(8,128)(2,1)S(1)}, u32[]{:S(2)}, u32[]{:S(2)}) collective-permute-start(bf16[144,1024]{1,0:T(8,128)(2,1)S(1)} %get-tuple-element.40.after_ref), channel_id=1, source_target_pairs={{0,8},{1,9},{2,10},{3,11},{4,12},{5,13},{6,14},{7,15},{8,0},{9,1},... | collective-permute-start | bytes 884744 | tf_op jit(solution)/shard_map/ppermute | solution.py:48
  18.2 2.9 %collective-permute-start.9 = (bf16[128,1024]{1,0:T(8,128)(2,1)S(1)}, bf16[128,1024]{1,0:T(8,128)(2,1)S(1)}, u32[]{:S(2)}, u32[]{:S(2)}) collective-permute-start(bf16[128,1024]{1,0:T(8,128)(2,1)S(1)} %shard_map.127), channel_id=1, source_target_pairs={{0,8},{1,9},{2,10},{3,11},{4,12},{5,13},{6,14},{7,15},{8,0},{9,1},... | collective-permute-start | bytes 786440 | tf_op jit(solution)/shard_map/ppermute | solution.py:48
  19.7 6.4 %collective-permute-start.8 = (bf16[128,1024]{1,0:T(8,128)(2,1)S(1)}, bf16[128,1024]{1,0:T(8,128)(2,1)S(1)}, u32[]{:S(2)}, u32[]{:S(2)}) collective-permute-start(bf16[128,1024]{1,0:T(8,128)(2,1)S(1)} %shard_map.124.refs_6_), channel_id=1, source_target_pairs={{0,2},{1,3},{2,0},{3,1},{4,6},{5,7},{6,4},{7,5},{8,16},{9,17},{10,... | collective-permute-start | bytes 786440 | tf_op jit(solution)/shard_map/ppermute | solution.py:48
  21.2 7.8 %collective-permute-start.10 = (bf16[128,1024]{1,0:T(8,128)(2,1)S(1)}, bf16[128,1024]{1,0:T(8,128)(2,1)S(1)}, u32[]{:S(2)}, u32[]{:S(2)}) collective-permute-start(bf16[128,1024]{1,0:T(8,128)(2,1)S(1)} %shard_map.128.refs_6_), channel_id=1, source_target_pairs={{0,2},{1,3},{2,0},{3,1},{4,6},{5,7},{6,4},{7,5},{8,16},{9,17},{10,... | collective-permute-start | bytes 786440 | tf_op jit(solution)/shard_map/ppermute | solution.py:48
  29.0 6.8 %collective-permute-start.11 = (bf16[144,1024]{1,0:T(8,128)(2,1)S(1)}, bf16[144,1024]{1,0:T(8,128)(2,1)S(1)}, u32[]{:S(2)}, u32[]{:S(2)}) collective-permute-start(bf16[144,1024]{1,0:T(8,128)(2,1)S(1)} %get-tuple-element.45.after_ref), channel_id=1, source_target_pairs={{0,2},{1,3},{2,0},{3,1},{4,6},{5,7},{6,4},{7,5},{8,9},{9,8},{10,11... | collective-permute-start | bytes 884744 | tf_op jit(solution)/shard_map/ppermute | solution.py:48
  30.4 18.8 %collective-permute-start.13 = (bf16[128,1024]{1,0:T(8,128)(2,1)S(1)}, bf16[128,1024]{1,0:T(8,128)(2,1)S(1)}, u32[]{:S(2)}, u32[]{:S(2)}) collective-permute-start(bf16[128,1024]{1,0:T(8,128)(2,1)S(1)} %shard_map.133), channel_id=1, source_target_pairs={{0,2},{1,3},{2,0},{3,1},{4,6},{5,7},{6,4},{7,5},{8,9},{9,8},{10,11... | collective-permute-start | bytes 786440 | tf_op jit(solution)/shard_map/ppermute | solution.py:48
  35.8 21.7 %copy-start.4 = (bf16[1,128,2048]{2,1,0:T(8,128)(2,1)S(1)}, bf16[1,128,2048]{2,1,0:T(8,128)(2,1)}, u32[]{:S(2)}) copy-start(bf16[1,128,2048]{2,1,0:T(8,128)(2,1)} %param.14) | copy-start | bytes 1572868
  35.8 21.7 %copy-start.7 = (bf16[1,128,16]{1,2,0:T(8,128)(2,1)S(1)}, bf16[1,128,16]{1,2,0:T(8,128)(2,1)}, u32[]{:S(2)}) copy-start(bf16[1,128,16]{1,2,0:T(8,128)(2,1)} %param.15) | copy-start | bytes 12292
  35.8 16.3 %collective-permute-start.12 = (bf16[128,1024]{1,0:T(8,128)(2,1)S(1)}, bf16[128,1024]{1,0:T(8,128)(2,1)S(1)}, u32[]{:S(2)}, u32[]{:S(2)}) collective-permute-start(bf16[128,1024]{1,0:T(8,128)(2,1)S(1)} %shard_map.131.refs_7_), channel_id=1, source_target_pairs={{0,8},{1,9},{2,10},{3,11},{4,12},{5,13},{6,14},{7,15},{8,0},{9,1},... | collective-permute-start | bytes 786440 | tf_op jit(solution)/shard_map/ppermute | solution.py:48
  49.3 4.3 %collective-permute-start.14 = (bf16[128,1024]{1,0:T(8,128)(2,1)S(1)}, bf16[128,1024]{1,0:T(8,128)(2,1)S(1)}, u32[]{:S(2)}, u32[]{:S(2)}) collective-permute-start(bf16[128,1024]{1,0:T(8,128)(2,1)S(1)} %shard_map.134.refs_8_), channel_id=1, source_target_pairs={{0,8},{1,9},{2,10},{3,11},{4,12},{5,13},{6,14},{7,15},{8,0},{9,1},... | collective-permute-start | bytes 786440 | tf_op jit(solution)/shard_map/ppermute | solution.py:48
  53.8 3.6 %collective-permute-start.15 = (bf16[16,128]{1,0:T(8,128)(2,1)S(1)}, bf16[16,128]{1,0:T(8,128)(2,1)S(1)}, u32[]{:S(2)}, u32[]{:S(2)}) collective-permute-start(bf16[16,128]{1,0:T(8,128)(2,1)S(1)} %get-tuple-element.48.after_ref.refs_4_), channel_id=1, source_target_pairs={{0,1},{1,0},{2,3},{3,2},{4,5},{5,4},{6,7},{7,6},{8,9},{9,8},{10,11... | collective-permute-start | bytes 12296 | tf_op jit(solution)/shard_map/ppermute | solution.py:48
  57.7 6.2 %collective-permute-start.17 = (bf16[16,2048]{1,0:T(8,128)(2,1)S(1)}, bf16[16,2048]{1,0:T(8,128)(2,1)S(1)}, u32[]{:S(2)}, u32[]{:S(2)}) collective-permute-start(bf16[16,2048]{1,0:T(8,128)(2,1)S(1)} %get-tuple-element.51), channel_id=1, source_target_pairs={{0,4},{1,5},{2,6},{3,7},{4,0},{5,1},{6,2},{7,3},{8,12},{9,13},{10,... | collective-permute-start | bytes 196616 | tf_op jit(solution)/shard_map/ppermute | solution.py:48
  62.4 9.2 %collective-permute-start.16 = (bf16[128,2048]{1,0:T(8,128)(2,1)S(1)}, bf16[128,2048]{1,0:T(8,128)(2,1)S(1)}, u32[]{:S(2)}, u32[]{:S(2)}) collective-permute-start(bf16[128,2048]{1,0:T(8,128)(2,1)S(1)} %shard_map.138), channel_id=1, source_target_pairs={{0,1},{1,0},{2,3},{3,2},{4,5},{5,4},{6,7},{7,6},{8,10},{9,11},{10,... | collective-permute-start | bytes 1572872 | tf_op jit(solution)/shard_map/ppermute | solution.py:48
  64.0 5.0 %collective-permute-start.18 = (bf16[8,2048]{1,0:T(8,128)(2,1)S(1)}, bf16[8,2048]{1,0:T(8,128)(2,1)S(1)}, u32[]{:S(2)}, u32[]{:S(2)}) collective-permute-start(bf16[8,2048]{1,0:T(8,128)(2,1)S(1)} %get-tuple-element.53), channel_id=1, source_target_pairs={{0,2},{1,3},{2,0},{3,1},{4,6},{5,7},{6,4},{7,5},{8,10},{9,11},{10,... | collective-permute-start | bytes 98312 | tf_op jit(solution)/shard_map/ppermute | solution.py:48
